TPU v7x, 32 devices: a whole 2x2x4 slice. The times are simulated.
32 devices in a mesh: layer: 4 (over y, x), row: 4 (over z), col: 2 (over core).
Axes of the slice: x: 2, y: 2, z: 4, core: 2. Of those that a mesh axis runs over, the one named last changes fastest.
Arguments:
- density: bfloat16 [2048, 2048], P('row', 'col'), may hold values from -0.5 to 1.5
- pattern: int32 [16, 16], P('row', 'col'), may hold values from 0 to 1, as said below
- holder: int32 [1024, 1], P(('layer', 'row', 'col')), may hold values from 0 to 7; in each aligned block of 32 rows (0 to 31, 32 to 63, ...) at most 8 rows name the same one
- slot_index: int32 [1024], P(('layer', 'row', 'col')), may hold values from 0 to 7
- atom_index: int32 [1024], P(('layer', 'row', 'col')), may hold values from 0 to 7
- derivative: bfloat16 [1024, 3, 128, 128], P(('layer', 'row', 'col')), may hold values from -1.1953125 to 1.1953125
Outputs:
- forces: float32 [3, 256], P(None, ('layer', 'row', 'col'))
Inputs may be any that keep to these rules, and one draw needn't show every extreme that they name: `pattern`: the blocks held by one (row, col) grid position form a tile of 4 x 8; in some tile every block is 1. Among the derivative blocks of one device no holder is named more than 8 times, a bound that some block reaches; every holder is named on some device.
All inputs are finite; a program needn't handle non-finite values.
Results may differ from a plain program's by a relative error of at most 0.015.
Values may be sent and summed in bfloat16 or wider, within the bound.
No kernel may reach another device: no remote copies, remote signals or barrier semaphores. Data moves between devices by JAX's collectives and lax.ppermute only.
A program may use at most 128 MiB of HBM per device.

v0:
```python
import functools

import jax
import jax.numpy as jnp
from jax import lax
from jax.experimental import pallas as pl
from jax.experimental.pallas import tpu as pltpu
from jax.sharding import PartitionSpec as P


BS = 128
ATOM_DEV = 8
RESIDENT_GRID = (4, 4, 2)
ALONG_X, ALONG_Y = 1, 2


def block_filter(matrix, kept_blocks):
    count_rows, count_cols = kept_blocks.shape
    blocked = matrix.reshape(count_rows, BS, count_cols, BS)
    return jnp.where(kept_blocks[:, None, :, None], blocked, jnp.zeros_like(blocked)).reshape(
        matrix.shape
    )


def column_subset(matrix, layer_count, layer_id):
    reshaped = matrix.reshape(matrix.shape[0], -1, layer_count, BS)
    picked = lax.dynamic_index_in_dim(reshaped, layer_id, 2, keepdims=False)
    return picked.reshape(matrix.shape[0], -1)


def row_subset(matrix, layer_count, layer_id):
    reshaped = matrix.reshape(-1, layer_count, BS, matrix.shape[1])
    picked = lax.dynamic_index_in_dim(reshaped, layer_id, 1, keepdims=False)
    return picked.reshape(-1, matrix.shape[1])


def multiply(left_matrix, right_matrix, layer_count, layer_id):
    left_part = column_subset(left_matrix, layer_count, layer_id)
    right_part = row_subset(right_matrix, layer_count, layer_id)
    row_strip = lax.all_gather(right_part, "row", axis=0, tiled=True)
    return jnp.dot(
        lax.all_gather(left_part, "col", axis=1, tiled=True),
        row_strip,
        preferred_element_type=jnp.float32,
    )


def split_shards(density, pattern, holder, slot_index, atom_index, derivative):
    layer_count = lax.axis_size("layer")
    layer_id = lax.axis_index("layer")
    grid_row = lax.axis_index("row")
    grid_col = lax.axis_index("col")
    row_blocks, col_blocks = pattern.shape
    global_rows = grid_row * row_blocks + jnp.arange(row_blocks, dtype=jnp.int32)
    global_cols = grid_col * col_blocks + jnp.arange(col_blocks, dtype=jnp.int32)
    kept_blocks = (pattern == 1) | (global_rows[:, None] == global_cols[None, :])
    filtered = block_filter(density, kept_blocks)
    partial_square = multiply(filtered, filtered, layer_count, layer_id)
    share_blocks = row_blocks // layer_count
    square_share = lax.psum_scatter(
        partial_square, "layer", scatter_dimension=0, tiled=True
    ).astype(jnp.bfloat16)
    square = lax.all_gather(square_share, "layer", axis=0, tiled=True)
    partial_cube = multiply(square, filtered, layer_count, layer_id)
    cube_share = lax.psum_scatter(partial_cube, "layer", scatter_dimension=0, tiled=True)
    kept_share = lax.dynamic_slice_in_dim(kept_blocks, layer_id * share_blocks, share_blocks, 0)
    purified = block_filter(
        3.0 * square_share.astype(jnp.float32) - 2.0 * cube_share, kept_share
    ).astype(jnp.bfloat16)
    held_blocks = (
        purified.reshape(share_blocks, BS, col_blocks, BS)
        .transpose(0, 2, 1, 3)
        .reshape(share_blocks * col_blocks, BS, BS)
    )
    holders_total = lax.axis_size("row") * lax.axis_size("col")
    entry_count = slot_index.shape[0]
    capacity = max(2, 2 * entry_count // holders_total)
    targets = holder[:, 0]
    target_hot = (targets[:, None] == jnp.arange(holders_total, dtype=jnp.int32)[None, :]).astype(
        jnp.int32
    )
    rank_values = jnp.sum(target_hot * (jnp.cumsum(target_hot, axis=0) - 1), axis=1)
    positions = targets * capacity + rank_values
    position_hot = (
        positions[None, :] == jnp.arange(holders_total * capacity, dtype=jnp.int32)[:, None]
    )
    requests = jnp.sum(jnp.where(position_hot, slot_index[None, :], 0), axis=1).reshape(
        holders_total, capacity
    )
    fetched = jnp.take(
        held_blocks,
        lax.all_to_all(requests, ("row", "col"), split_axis=0, concat_axis=0, tiled=True),
        axis=0,
    )
    returned = lax.all_to_all(fetched, ("row", "col"), split_axis=0, concat_axis=0, tiled=True)
    arrived = jnp.take(returned.reshape(holders_total * capacity, BS, BS), positions, axis=0)
    contrib = jnp.einsum("eij,exij->xe", arrived, derivative, preferred_element_type=jnp.float32)
    atom_hot = (atom_index[:, None] == jnp.arange(ATOM_DEV, dtype=jnp.int32)[None, :]).astype(
        jnp.float32
    )
    return -2.0 * jnp.dot(contrib, atom_hot, precision=lax.Precision.HIGHEST)


def positions_of():
    return lax.axis_index("layer"), lax.axis_index("row"), lax.axis_index("col")


def kept_block(pattern_ref, row, column, grid_row, grid_col):
    row_blocks, col_blocks = pattern_ref.shape
    diagonal = grid_row * row_blocks + row == grid_col * col_blocks + column
    return (pattern_ref[row, column] == 1) | diagonal


def clear_blocks(out, pattern_ref, first, count, grid_row, grid_col):
    for i in range(count):
        for q in range(pattern_ref.shape[1]):
            kept = kept_block(pattern_ref, first + i, q, grid_row, grid_col)

            @pl.when(jnp.logical_not(kept))
            def _():
                out[i * BS : (i + 1) * BS, q * BS : (q + 1) * BS] = jnp.zeros((BS, BS), out.dtype)


def unit_kernel(share, density_ref, source_ref, out_ref, pattern_ref, sems):
    layer_id, grid_row, grid_col = positions_of()
    rows = share * BS
    copies = []
    begin(copies, source_ref, pattern_ref, sems.at[0])
    start = pl.multiple_of(layer_id * rows, rows)
    begin(copies, density_ref.at[pl.ds(start, rows), :], out_ref, sems.at[1])
    for copy in copies:
        copy.wait()
    clear_blocks(out_ref, pattern_ref, layer_id * share, share, grid_row, grid_col)


def filter_kernel(share, far, density_ref, *refs):
    source_refs, refs = refs[:-6], refs[-6:]
    out_ref, far_ref, full, patterns_ref, pattern_ref, sems = refs
    layer_id, grid_row, grid_col = positions_of()
    rows = share * BS
    unit = layer_id ^ far
    row_blocks, col_blocks = pattern_ref.shape
    own = full.at[
        pl.ds(pl.multiple_of(grid_row * row_blocks * BS, row_blocks * BS), row_blocks * BS),
        pl.ds(pl.multiple_of(grid_col * col_blocks * BS, col_blocks * BS), col_blocks * BS),
    ]
    copies = []
    begin(copies, source_refs[0], pattern_ref, sems.at[0])
    for k, ref in enumerate(source_refs):
        begin(copies, ref, patterns_ref.at[k], sems.at[4 + k])
    begin(copies, density_ref, out_ref, sems.at[1])
    begin(copies, density_ref, own, sems.at[2])
    start = pl.multiple_of(unit * rows, rows)
    begin(copies, density_ref.at[pl.ds(start, rows), :], far_ref, sems.at[3])
    for copy in copies:
        copy.wait()
    clear_blocks(far_ref, pattern_ref, unit * share, share, grid_row, grid_col)
    for out in (out_ref, own):
        clear_blocks(out, pattern_ref, 0, row_blocks, grid_row, grid_col)


def begin(copies, source, target, sem):
    copies.append(pltpu.make_async_copy(source, target, sem))
    copies[-1].start()


def flip_of(kind, core):
    if kind == "a":
        return ALONG_X + core * (ALONG_Y - ALONG_X)
    if kind == "b":
        return ALONG_Y + core * (ALONG_X - ALONG_Y)
    return kind


def unit_start(layer_id, grid_row, core, unit, row_blocks, rows):
    d, kind = unit
    first = (grid_row ^ d) * row_blocks * BS
    return first if kind is None else first + (layer_id ^ flip_of(kind, core)) * rows


def square_kernel(layout, pairs, absent, share, row_blocks, col_blocks, *refs):
    count = len(layout)
    unit_refs, refs = refs[:count], refs[count:]
    first = len(refs) == 6
    if first:
        _, full, left, partial, sems, left_sems = refs
    else:
        _, _, left, full, partial, sems, left_sems = refs
    layer_id, grid_row, grid_col = positions_of()
    rows = share * BS
    width = col_blocks * BS
    copies = []
    for slot, (ref, (unit, half, placed)) in enumerate(zip(unit_refs, layout)):
        core = grid_col ^ half
        columns = pl.ds(pl.multiple_of(core * width, width), width)
        if not placed:
            height = ref.shape[0]
            start = unit_start(layer_id, grid_row, core, unit, row_blocks, rows)
            start = pl.multiple_of(start, height)
            begin(copies, ref, full.at[pl.ds(start, height), columns], sems.at[slot])
        if first and not unit[1]:
            source = ref
            if unit[1] is None:
                source = ref.at[pl.ds(pl.multiple_of(layer_id * rows, rows), rows), :]
            start = pl.multiple_of((grid_row ^ unit[0]) * rows, rows)
            begin(copies, source, left.at[pl.ds(start, rows), columns], left_sems.at[slot])
    for unit in absent:
        start = unit_start(layer_id, grid_row, grid_col, unit, row_blocks, rows)
        full[pl.ds(pl.multiple_of(start, rows), rows), :] = jnp.zeros(
            (rows, full.shape[1]), full.dtype
        )
    for copy in copies:
        copy.wait()
    depth = 2 * rows
    total = None if first else partial[...]
    for d, flip in pairs:
        start = (grid_row ^ d) * row_blocks * BS + (layer_id ^ flip) // 2 * depth
        k = pl.ds(pl.multiple_of(start, depth), depth)
        more = jnp.dot(left[:, k], full[k, :], preferred_element_type=jnp.float32)
        total = more if total is None else total + more
    partial[...] = total


def force_kernel(late, absent, n_rows, n_cols, share, row_blocks, col_blocks, *refs):
    tables, refs = refs[:5], refs[5:]
    late_refs, refs = refs[: len(late)], refs[len(late) :]
    (
        full_ref,
        left,
        partial,
        held,
        forces_ref,
        full,
        square,
        purified,
        last,
        last_left,
        totals,
        kept,
        holder_ref,
        slot_ref,
        atom_ref,
        patterns_ref,
        sems,
        table_sems,
    ) = refs
    del full_ref
    layer_id, grid_row, grid_col = positions_of()
    rows = share * BS
    width = col_blocks * BS
    copies = []
    for k, (ref, (unit, half)) in enumerate(zip(late_refs, late)):
        core = grid_col ^ half
        column = pl.multiple_of(core * width, width)
        place = absent.index(unit) * rows
        begin(copies, ref, last.at[pl.ds(place, rows), pl.ds(column, width)], sems.at[k])
    places = [holder_ref, slot_ref, atom_ref, patterns_ref.at[0], patterns_ref.at[1]]
    table_copies = []
    for k, (table, place) in enumerate(zip(tables, places)):
        begin(table_copies, table, place, table_sems.at[k])
    totals[...] = jnp.zeros_like(totals)
    starts = [
        pl.multiple_of(unit_start(layer_id, grid_row, grid_col, unit, row_blocks, rows), rows)
        for unit in absent
    ]
    for k, start in enumerate(starts):
        last_left[:, k * rows : (k + 1) * rows] = left[:, pl.ds(start, rows)]
    for copy in copies:
        copy.wait()
    for k, start in enumerate(starts):
        full[pl.ds(start, rows), :] = last[k * rows : (k + 1) * rows, :]
    more = jnp.dot(last_left[...], last[...], preferred_element_type=jnp.float32)
    square[...] = (partial[...] + more).astype(square.dtype)
    cube = jnp.dot(square[...], full[...], preferred_element_type=jnp.float32)
    purified[...] = (3.0 * square[...].astype(jnp.float32) - 2.0 * cube).astype(purified.dtype)

    for copy in table_copies:
        copy.wait()
    for half in range(2):
        for d in range(n_rows):
            pattern_ref = patterns_ref.at[half, d]
            place, column = grid_row ^ d, grid_col ^ half
            for i in range(share):
                for q in range(col_blocks):
                    value = kept_block(pattern_ref, layer_id * share + i, q, place, column)
                    kept[place * share + i, column * col_blocks + q] = value.astype(jnp.int32)

    @pl.loop(0, held.shape[0], unroll=4)
    def _(e):
        h = holder_ref[e]
        s = slot_ref[e]
        row = (h // n_cols) * share + s // col_blocks
        column = (h % n_cols) * col_blocks + s % col_blocks
        block = purified[
            pl.ds(pl.multiple_of(row * BS, BS), BS), pl.ds(pl.multiple_of(column * BS, BS), BS)
        ].astype(jnp.float32)

        keep = kept[row, column] == 1
        for x in range(held.shape[1]):
            product = block * held[e, x].astype(jnp.float32)
            part = jnp.sum(product.reshape(BS // 8, 8, BS), axis=0)
            part = jnp.where(keep, part, jnp.zeros_like(part))
            totals[x, atom_ref[e]] = totals[x, atom_ref[e]] + part

    sums = jnp.sum(jnp.sum(totals[...], axis=3), axis=2)
    forces_ref[...] = -2.0 * sums


VMEM = pl.BlockSpec(memory_space=pltpu.VMEM)
SMEM = pl.BlockSpec(memory_space=pltpu.SMEM)
ANY = pl.BlockSpec(memory_space=pl.ANY)
HBM = pl.BlockSpec(memory_space=pltpu.HBM)


def resident_step(sizes, density, pattern, holder, slot_index, atom_index, derivative):
    layers, n_rows, n_cols = sizes
    row_blocks, col_blocks = pattern.shape
    share = row_blocks // layers
    rows = share * BS
    width = n_cols * col_blocks * BS
    height = n_rows * row_blocks * BS
    tall = n_rows * rows
    dtype = density.dtype
    grid_row = lax.axis_index("row")
    outer = n_rows - 1
    inner = (grid_row != 0) & (grid_row != outer)
    middle = tuple(range(1, outer))

    def send(value, axis, flip, only=None):
        pairs = [
            (i, i ^ flip) for i in range(lax.axis_size(axis)) if only is None or i in only
        ]
        return lax.ppermute(value, axis, pairs)

    def spread(value, kind):
        pairs = [
            (g * n_cols + c, (g ^ flip_of(kind, c)) * n_cols + c)
            for g in range(layers)
            for c in range(n_cols)
        ]
        return lax.ppermute(value, ("layer", "col"), pairs)

    masks = pltpu.SMEM(pattern.shape, pattern.dtype)
    full_shape = jax.ShapeDtypeStruct((height, width), dtype)
    unit_shape = jax.ShapeDtypeStruct((rows, density.shape[1]), dtype)
    near = pl.pallas_call(
        functools.partial(unit_kernel, share),
        out_shape=unit_shape,
        in_specs=[ANY, ANY],
        out_specs=VMEM,
        scratch_shapes=[masks, pltpu.SemaphoreType.DMA((2,))],
        name="unit",
    )(density, pattern)
    filter_call = pl.pallas_call(
        functools.partial(filter_kernel, share, ALONG_X ^ ALONG_Y),
        out_shape=[
            jax.ShapeDtypeStruct(density.shape, dtype),
            unit_shape,
            full_shape,
            jax.ShapeDtypeStruct((n_rows,) + pattern.shape, pattern.dtype),
        ],
        in_specs=[ANY] * (1 + n_rows),
        out_specs=[VMEM] * 4,
        scratch_shapes=[masks, pltpu.SemaphoreType.DMA((4 + n_rows,))],
        compiler_params=pltpu.CompilerParams(vmem_limit_bytes=16 * 2**20),
        name="filter",
    )
    patterns = [pattern] + [send(pattern, "row", d) for d in range(1, n_rows)]
    filtered, far, full, patterns = filter_call(density, *patterns)
    other_patterns = send(patterns, "col", 1)
    other = send(filtered, "col", 1)

    z1 = send(near, "row", 1)
    b = send(near, "row", outer, middle)
    d = send(z1, "row", outer, middle)
    c = send(b, "row", 1, middle)
    e = send(d, "row", 1, middle)
    z2 = jnp.where(inner, d, c)
    z3 = jnp.where(inner, b, e)

    diagonal = ALONG_X ^ ALONG_Y
    absent = ((3, diagonal),)
    placed = [((0, 0), 0, True, near), ((0, None), 1, False, other)]
    late = []
    for k, z in ((1, z1), (2, z2), (3, z3)):
        a_ = spread(z, "a")
        b_ = spread(z, "b")
        w_ = send(far, "row", 1) if k == 1 else spread(a_, "b")
        for kind, value in ((0, z), ("a", a_), ("b", b_), (diagonal, w_)):
            partner = send(value, "col", 1)
            for half, part in enumerate((value, partner)):
                if (k, kind) in absent:
                    late.append(((k, kind), half, part))
                else:
                    placed.append(((k, kind), half, False, part))
    left_shape = jax.ShapeDtypeStruct((tall, width), dtype)
    partial_shape = jax.ShapeDtypeStruct((tall, width), jnp.float32)

    def add_squares(units, pairs, zeros, full, *held):
        count = len(units)
        layout = tuple(u[:3] for u in units)
        return pl.pallas_call(
            functools.partial(square_kernel, layout, pairs, zeros, share, row_blocks, col_blocks),
            out_shape=[full_shape] + ([] if held else [left_shape]) + [partial_shape],
            in_specs=[HBM] * count + [VMEM] * (1 + len(held)),
            out_specs=[VMEM] * (2 if held else 3),
            input_output_aliases={count: 0, count + 1: 1} if held else {count: 0},
            scratch_shapes=[pltpu.SemaphoreType.DMA((count,))] * 2,
            compiler_params=pltpu.CompilerParams(vmem_limit_bytes=24 * 2**20),
        )(*[u[3] for u in units], full, *held)

    behind = ((1, diagonal), (2, diagonal), (3, "a"), (3, "b"))
    early = [u for u in placed if u[0] not in behind]
    later = [u for u in placed if u[0] in behind]
    full, left, partial = add_squares(early, ((0, 0), (0, ALONG_Y), (1, 0), (2, 0)), (), full)
    full, partial = add_squares(
        later, ((1, ALONG_Y), (2, ALONG_Y), (3, 0), (3, ALONG_Y)), absent, full, partial, left
    )
    tables = [holder.reshape(-1), slot_index, atom_index, patterns, other_patterns]
    n_late = len(late)
    components = derivative.shape[1]
    return pl.pallas_call(
        functools.partial(
            force_kernel,
            tuple(u[:2] for u in late),
            absent,
            n_rows,
            n_cols,
            share,
            row_blocks,
            col_blocks,
        ),
        out_shape=[jax.ShapeDtypeStruct((components, ATOM_DEV), jnp.float32), full_shape],
        in_specs=[ANY] * len(tables) + [HBM] * n_late + [VMEM] * 4,
        out_specs=[VMEM] * 2,
        input_output_aliases={len(tables) + n_late: 1},
        scratch_shapes=[
            pltpu.VMEM((tall, width), dtype),
            pltpu.VMEM((tall, width), dtype),
            pltpu.VMEM((len(absent) * rows, width), dtype),
            pltpu.VMEM((tall, len(absent) * rows), dtype),
            pltpu.VMEM((components, ATOM_DEV, 8, BS), jnp.float32),
            pltpu.SMEM((n_rows * share, n_cols * col_blocks), jnp.int32),
            pltpu.SMEM(slot_index.shape, jnp.int32),
            pltpu.SMEM(slot_index.shape, jnp.int32),
            pltpu.SMEM(slot_index.shape, jnp.int32),
            pltpu.SMEM((2, n_rows) + pattern.shape, jnp.int32),
            pltpu.SemaphoreType.DMA((n_late,)),
            pltpu.SemaphoreType.DMA((len(tables),)),
        ],
        compiler_params=pltpu.CompilerParams(vmem_limit_bytes=24 * 2**20),
        name="force",
    )(*tables, *[u[2] for u in late], full, left, partial, derivative)[0]


def resident_fits(mesh):
    return tuple(mesh.shape[axis] for axis in ("layer", "row", "col")) == RESIDENT_GRID


def solution(mesh):
    specs = dict(
        mesh=mesh,
        in_specs=(
            P("row", "col"),
            P("row", "col"),
            P(("layer", "row", "col"), None),
            P(("layer", "row", "col")),
            P(("layer", "row", "col")),
            P(("layer", "row", "col"), None, None, None),
        ),
        out_specs=P(None, ("layer", "row", "col")),
        check_vma=False,
    )
    if not resident_fits(mesh):
        return jax.shard_map(split_shards, **specs)
    sizes = tuple(mesh.shape[axis] for axis in ("layer", "row", "col"))

    def shards(*args):
        return resident_step(sizes, *args)

    return jax.shard_map(shards, **specs)
```

profile of v0, /device:TPU:0, one launch (start us, length us, event | category | flops | bytes accessed | tf_op | source)
XLA Modules:
  0.0 82.1 jit_solution(9970933185363229616)
XLA Ops:
  0.0 1.7 %unit.1.refs_0_ = bf16[128,1024]{1,0:T(8,128)(2,1)} custom-call(bf16[512,1024]{1,0:T(8,128)(2,1)} %density_ref.3, s32[4,8]{1,0:T(4,128)} %source_ref.1), custom_call_target="tpu_custom_call" | custom-call | tf_op jit(solution)/shard_map/unit/pallas_call | solution.py:346
  1.7 3.1 %collective-permute-start.5 = (bf16[128,1024]{1,0:T(8,128)(2,1)}, bf16[128,1024]{1,0:T(8,128)(2,1)S(1)}, u32[]{:S(2)}, u32[]{:S(2)}) collective-permute-start(bf16[128,1024]{1,0:T(8,128)(2,1)} %unit.1.refs_0_), channel_id=1, source_target_pairs={{0,2},{2,0},{4,6},{6,4},{1,3},{3,1},{5,7},{7,5},{8,10},{10,8},{12,... | collective-permute-start | bytes 786440 | tf_op jit(solution)/shard_map/ppermute | solution.py:333
  4.9 0.7 collective-permute-start.4
  5.5 4.4 %collective-permute-start = (s32[4,8]{1,0:T(4,128)}, s32[4,8]{1,0:T(4,128)S(1)}, u32[]{:S(2)}, u32[]{:S(2)}) collective-permute-start(s32[4,8]{1,0:T(4,128)} %source_ref.1), channel_id=1, source_target_pairs={{0,2},{2,0},{4,6},{6,4},{1,3},{3,1},{5,7},{7,5},{8,10},{10,8},{12,... | collective-permute-start | bytes 392 | tf_op jit(solution)/shard_map/ppermute | solution.py:333
  9.9 0.0 collective-permute-start.1
  9.9 2.4 %collective-permute-start.2 = (s32[4,8]{1,0:T(4,128)}, s32[4,8]{1,0:T(4,128)S(1)}, u32[]{:S(2)}, u32[]{:S(2)}) collective-permute-start(s32[4,8]{1,0:T(4,128)} %source_ref.1), channel_id=1, source_target_pairs={{0,6},{2,4},{4,2},{6,0},{1,7},{3,5},{5,3},{7,1},{8,14},{10,12},{12... | collective-permute-start | bytes 392 | tf_op jit(solution)/shard_map/ppermute | solution.py:333
  12.4 3.3 %collective-permute-done.1.refs_2_ = s32[4,8]{1,0:T(4,128)S(1)} collective-permute-done((s32[4,8]{1,0:T(4,128)}, s32[4,8]{1,0:T(4,128)S(1)}, u32[]{:S(2)}, u32[]{:S(2)}) %collective-permute-start.1) | collective-permute-done | bytes 160 | tf_op jit(solution)/shard_map/ppermute | solution.py:333
  15.7 0.0 collective-permute-done.2.refs_3_
  15.7 1.2 %copy-done.2 = bf16[512,1024]{1,0:T(8,128)(2,1)S(1)} copy-done((bf16[512,1024]{1,0:T(8,128)(2,1)S(1)}, bf16[512,1024]{1,0:T(8,128)(2,1)}, u32[]{:S(2)}) %copy-start.2) | copy-done | bytes 1048600
  16.9 0.7 copy-done.5
  17.6 1.3 %filter.1 = (bf16[512,1024]{1,0:T(8,128)(2,1)S(1)}, bf16[128,1024]{1,0:T(8,128)(2,1)S(1)}, bf16[2048,2048]{1,0:T(8,128)(2,1)S(1)}, s32[4,4,8]{2,1,0:T(4,128)S(1)}) custom-call(bf16[512,1024]{1,0:T(8,128)(2,1)S(1)} %copy-done.2, s32[4,8]{1,0:T(4,128)S(1)} %copy-done.5, s32[4,8]{1,0:T(4,128)S(1)} %collective-permute-done.refs_1_, ...), custom_call_target="tpu_custom_call" | custom-call | tf_op jit(solution)/shard_map/filter/pallas_call | solution.py:369
  18.9 3.3 %copy-done = bf16[2048,2048]{1,0:T(8,128)(2,1)} copy-done((bf16[2048,2048]{1,0:T(8,128)(2,1)}, bf16[2048,2048]{1,0:T(8,128)(2,1)S(1)}, u32[]{:S(2)}) %copy-start) | copy-done | bytes 8388632
  22.2 0.6 collective-permute-start.11
  22.8 0.0 collective-permute-done.5.refs_2_
  22.8 0.7 collective-permute-start.6
  23.4 1.3 %collective-permute-start.13 = (bf16[128,1024]{1,0:T(8,128)(2,1)S(1)}, bf16[128,1024]{1,0:T(8,128)(2,1)S(1)}, u32[]{:S(2)}, u32[]{:S(2)}) collective-permute-start(bf16[128,1024]{1,0:T(8,128)(2,1)S(1)} %collective-permute-done.4), channel_id=1, source_target_pairs={{2,0},{4,6},{3,1},{5,7},{10,8},{12,14},{11,9},{13,15},{18,16},{20,... | collective-permute-start | bytes 786440 | tf_op jit(solution)/shard_map/ppermute | solution.py:333
  24.8 1.5 %collective-permute-start.22 = (bf16[128,1024]{1,0:T(8,128)(2,1)S(1)}, bf16[128,1024]{1,0:T(8,128)(2,1)S(1)}, u32[]{:S(2)}, u32[]{:S(2)}) collective-permute-start(bf16[128,1024]{1,0:T(8,128)(2,1)S(1)} %collective-permute-done.5.refs_2_), channel_id=1, source_target_pairs={{0,8},{1,17},{8,0},{9,25},{16,24},{17,1},{24,16},{25,9},{2,10},{3,... | collective-permute-start | bytes 786440 | tf_op jit(solution)/shard_map/ppermute | solution.py:341
  26.3 1.5 %collective-permute-start.24 = (bf16[128,1024]{1,0:T(8,128)(2,1)S(1)}, bf16[128,1024]{1,0:T(8,128)(2,1)S(1)}, u32[]{:S(2)}, u32[]{:S(2)}) collective-permute-start(bf16[128,1024]{1,0:T(8,128)(2,1)S(1)} %collective-permute-done.5.refs_2_), channel_id=1, source_target_pairs={{0,16},{1,9},{8,24},{9,1},{16,0},{17,25},{24,8},{25,17},{2,18},{3,... | collective-permute-start | bytes 786440 | tf_op jit(solution)/shard_map/ppermute | solution.py:341
  27.8 2.4 %collective-permute-done.11.refs_0_ = bf16[128,1024]{1,0:T(8,128)(2,1)S(1)} collective-permute-done((bf16[128,1024]{1,0:T(8,128)(2,1)S(1)}, bf16[128,1024]{1,0:T(8,128)(2,1)S(1)}, u32[]{:S(2)}, u32[]{:S(2)}) %collective-permute-start.11) | collective-permute-done | bytes 262176 | tf_op jit(solution)/shard_map/ppermute | solution.py:333
  30.2 0.5 collective-permute-start.12
  30.7 3.9 %collective-permute-done.13 = bf16[128,1024]{1,0:T(8,128)(2,1)S(1)} collective-permute-done((bf16[128,1024]{1,0:T(8,128)(2,1)S(1)}, bf16[128,1024]{1,0:T(8,128)(2,1)S(1)}, u32[]{:S(2)}, u32[]{:S(2)}) %collective-permute-start.13) | collective-permute-done | bytes 262176 | tf_op jit(solution)/shard_map/ppermute | solution.py:333
  34.7 1.5 %collective-permute-start.14 = (bf16[128,1024]{1,0:T(8,128)(2,1)S(1)}, bf16[128,1024]{1,0:T(8,128)(2,1)S(1)}, u32[]{:S(2)}, u32[]{:S(2)}) collective-permute-start(bf16[128,1024]{1,0:T(8,128)(2,1)S(1)} %broadcast_select_fusion.refs_8_), channel_id=1, source_target_pairs={{0,8},{1,17},{8,0},{9,25},{16,24},{17,1},{24,16},{25,9},{2,10},{3,... | collective-permute-start | bytes 786440 | tf_op jit(solution)/shard_map/ppermute | solution.py:341
  36.2 0.0 collective-permute-done.22.refs_4_
  36.2 1.5 %collective-permute-start.28 = (bf16[128,1024]{1,0:T(8,128)(2,1)S(1)}, bf16[128,1024]{1,0:T(8,128)(2,1)S(1)}, u32[]{:S(2)}, u32[]{:S(2)}) collective-permute-start(bf16[128,1024]{1,0:T(8,128)(2,1)S(1)} %broadcast_select_fusion.refs_8_), channel_id=1, source_target_pairs={{0,16},{1,9},{8,24},{9,1},{16,0},{17,25},{24,8},{25,17},{2,18},{3,... | collective-permute-start | bytes 786440 | tf_op jit(solution)/shard_map/ppermute | solution.py:341
  37.7 0.0 collective-permute-done.24.refs_6_
  37.7 0.0 collective-permute-start.26
  37.7 1.3 %collective-permute-start.7 = (bf16[128,1024]{1,0:T(8,128)(2,1)S(1)}, bf16[128,1024]{1,0:T(8,128)(2,1)S(1)}, u32[]{:S(2)}, u32[]{:S(2)}) collective-permute-start(bf16[128,1024]{1,0:T(8,128)(2,1)S(1)} %collective-permute-done.6), channel_id=1, source_target_pairs={{2,0},{4,6},{3,1},{5,7},{10,8},{12,14},{11,9},{13,15},{18,16},{20,... | collective-permute-start | bytes 786440 | tf_op jit(solution)/shard_map/ppermute | solution.py:333
  39.0 0.0 collective-permute-done.12.refs_1_
  39.0 0.6 collective-permute-start.20
  39.6 3.0 %collective-permute-done.14.refs_10_ = bf16[128,1024]{1,0:T(8,128)(2,1)S(1)} collective-permute-done((bf16[128,1024]{1,0:T(8,128)(2,1)S(1)}, bf16[128,1024]{1,0:T(8,128)(2,1)S(1)}, u32[]{:S(2)}, u32[]{:S(2)}) %collective-permute-start.14) | collective-permute-done | bytes 262176 | tf_op jit(solution)/shard_map/ppermute | solution.py:341
  42.6 0.0 collective-permute-start.23
  42.7 0.0 collective-permute-done.28.refs_12_
  42.7 0.5 collective-permute-start.25
  43.2 0.0 collective-permute-done.26.refs_9_
  43.2 0.1 collective-permute-start.27
  43.2 5.1 %collective-permute-done.7 = bf16[128,1024]{1,0:T(8,128)(2,1)S(1)} collective-permute-done((bf16[128,1024]{1,0:T(8,128)(2,1)S(1)}, bf16[128,1024]{1,0:T(8,128)(2,1)S(1)}, u32[]{:S(2)}, u32[]{:S(2)}) %collective-permute-start.7) | collective-permute-done | bytes 262176 | tf_op jit(solution)/shard_map/ppermute | solution.py:333
  48.3 0.0 collective-permute-start.29
  48.4 0.6 collective-permute-start.8
  49.0 0.2 collective-permute-start.30
  49.2 0.0 collective-permute-done.27.refs_11_
  49.2 1.5 %collective-permute-start.15 = (bf16[128,1024]{1,0:T(8,128)(2,1)S(1)}, bf16[128,1024]{1,0:T(8,128)(2,1)S(1)}, u32[]{:S(2)}, u32[]{:S(2)}) collective-permute-start(bf16[128,1024]{1,0:T(8,128)(2,1)S(1)} %collective-permute-done.14.refs_10_), channel_id=1, source_target_pairs={{0,16},{1,9},{8,24},{9,1},{16,0},{17,25},{24,8},{25,17},{2,18},{3,... | collective-permute-start | bytes 786440 | tf_op jit(solution)/shard_map/ppermute | solution.py:341
  50.7 0.0 collective-permute-done.29.refs_13_
  50.7 0.5 collective-permute-start.18
  51.2 6.3 %collective-permute-done.8.refs_4_ = bf16[128,1024]{1,0:T(8,128)(2,1)S(1)} collective-permute-done((bf16[128,1024]{1,0:T(8,128)(2,1)S(1)}, bf16[128,1024]{1,0:T(8,128)(2,1)S(1)}, u32[]{:S(2)}, u32[]{:S(2)}) %collective-permute-start.8) | collective-permute-done | bytes 262176 | tf_op jit(solution)/shard_map/ppermute | solution.py:341
  57.5 0.0 collective-permute-done.15.refs_2_
  57.6 0.5 collective-permute-start.16
  58.1 1.9 %collective-permute-done.18.refs_6_ = bf16[128,1024]{1,0:T(8,128)(2,1)S(1)} collective-permute-done((bf16[128,1024]{1,0:T(8,128)(2,1)S(1)}, bf16[128,1024]{1,0:T(8,128)(2,1)S(1)}, u32[]{:S(2)}, u32[]{:S(2)}) %collective-permute-start.18) | collective-permute-done | bytes 262176 | tf_op jit(solution)/shard_map/ppermute | solution.py:341
  60.0 0.3 collective-permute-start.19
  60.3 3.6 %collective-permute-done.9.refs_5_ = bf16[128,1024]{1,0:T(8,128)(2,1)S(1)} collective-permute-done((bf16[128,1024]{1,0:T(8,128)(2,1)S(1)}, bf16[128,1024]{1,0:T(8,128)(2,1)S(1)}, u32[]{:S(2)}, u32[]{:S(2)}) %collective-permute-start.9) | collective-permute-done | bytes 262176 | tf_op jit(solution)/shard_map/ppermute | solution.py:341
  63.9 0.0 collective-permute-start.10
  63.9 0.0 collective-permute-done.20.refs_1_
  63.9 0.5 collective-permute-start.3
  64.4 3.4 %copy-done.1 = bf16[2048,2048]{1,0:T(8,128)(2,1)S(1)} copy-done((bf16[2048,2048]{1,0:T(8,128)(2,1)S(1)}, bf16[2048,2048]{1,0:T(8,128)(2,1)}, u32[]{:S(2)}) %copy-start.1) | copy-done | bytes 8388632
  67.8 0.9 %copy-done.4 = bf16[128,1024]{1,0:T(8,128)(2,1)S(1)} copy-done((bf16[128,1024]{1,0:T(8,128)(2,1)S(1)}, bf16[128,1024]{1,0:T(8,128)(2,1)}, u32[]{:S(2)}) %copy-start.4) | copy-done | bytes 262168
  68.7 3.3 %shard_map.64 = (bf16[2048,2048]{1,0:T(8,128)(2,1)S(1)}, bf16[512,2048]{1,0:T(8,128)(2,1)S(1)}, f32[512,2048]{1,0:T(8,128)S(1)}) custom-call(bf16[128,1024]{1,0:T(8,128)(2,1)S(1)} %copy-done.4, bf16[512,1024]{1,0:T(8,128)(2,1)S(1)} %collective-permute-done.20.refs_1_, ...), custom_call_target="tpu_custom_call", output_to_operand_aliasing={{0}: (16, {})} | custom-call | tf_op jit(solution)/shard_map/pallas_call | solution.py:402
  72.1 0.0 collective-permute-done.17.refs_5_
  72.1 0.0 collective-permute-done.19.refs_7_
  72.1 0.0 copy-start.3
  72.1 0.0 copy-start.6
  72.1 0.0 copy-start.7
  72.1 0.0 copy-start.8
  72.2 2.8 %shard_map.65 = (bf16[2048,2048]{1,0:T(8,128)(2,1)S(1)}, f32[512,2048]{1,0:T(8,128)S(1)}) custom-call(bf16[128,1024]{1,0:T(8,128)(2,1)S(1)} %collective-permute-done.11.refs_0_, bf16[128,1024]{1,0:T(8,128)(2,1)S(1)} %collective-permute-done.12.refs_1_, ...), custom_call_target="tpu_custom_call", output_to_operand_aliasing={{0}: (8, {}), {1}: (9, {})} | custom-call | tf_op jit(solution)/shard_map/pallas_call | solution.py:402
  74.9 0.0 collective-permute-done.3.refs_4_
  75.0 7.2 %force.1 = (f32[3,8]{1,0:T(4,128)}, bf16[2048,2048]{1,0:T(8,128)(2,1)S(1)}) custom-call(s32[32]{0:T(128)S(1)} %bitcast.1, s32[32]{0:T(128)S(1)} %copy-done.7, s32[32]{0:T(128)S(1)} %copy-done.8, s32[4,4,8]{2,1,0:T(4,128)S(1)} %get-tuple-element.15.refs_3_, s32[4,4,8]{2,1,0:T(4,128)S(1)} %collective-permute-done.3.refs_4_, ...), custom_call_target="tpu_custom_call", output_to_operand_aliasing={{1}: (7, {})} | custom-call | tf_op jit(solution)/shard_map/force/pallas_call | solution.py:422
  (23 shorter events, 0.1 us)
Async XLA Ops:
  1.7 21.0 %collective-permute-start.5 = (bf16[128,1024]{1,0:T(8,128)(2,1)}, bf16[128,1024]{1,0:T(8,128)(2,1)S(1)}, u32[]{:S(2)}, u32[]{:S(2)}) collective-permute-start(bf16[128,1024]{1,0:T(8,128)(2,1)} %unit.1.refs_0_), channel_id=1, source_target_pairs={{0,2},{2,0},{4,6},{6,4},{1,3},{3,1},{5,7},{7,5},{8,10},{10,8},{12,... | collective-permute-start | bytes 786440 | tf_op jit(solution)/shard_map/ppermute | solution.py:333
  4.9 18.6 %collective-permute-start.4 = (bf16[128,1024]{1,0:T(8,128)(2,1)}, bf16[128,1024]{1,0:T(8,128)(2,1)S(1)}, u32[]{:S(2)}, u32[]{:S(2)}) collective-permute-start(bf16[128,1024]{1,0:T(8,128)(2,1)} %unit.1.refs_0_), channel_id=1, source_target_pairs={{2,4},{4,2},{3,5},{5,3},{10,12},{12,10},{11,13},{13,11},{18,20},{2... | collective-permute-start | bytes 786440 | tf_op jit(solution)/shard_map/ppermute | solution.py:333
  5.5 6.8 %collective-permute-start = (s32[4,8]{1,0:T(4,128)}, s32[4,8]{1,0:T(4,128)S(1)}, u32[]{:S(2)}, u32[]{:S(2)}) collective-permute-start(s32[4,8]{1,0:T(4,128)} %source_ref.1), channel_id=1, source_target_pairs={{0,2},{2,0},{4,6},{6,4},{1,3},{3,1},{5,7},{7,5},{8,10},{10,8},{12,... | collective-permute-start | bytes 392 | tf_op jit(solution)/shard_map/ppermute | solution.py:333
  9.9 5.8 %collective-permute-start.1 = (s32[4,8]{1,0:T(4,128)}, s32[4,8]{1,0:T(4,128)S(1)}, u32[]{:S(2)}, u32[]{:S(2)}) collective-permute-start(s32[4,8]{1,0:T(4,128)} %source_ref.1), channel_id=1, source_target_pairs={{0,4},{2,6},{4,0},{6,2},{1,5},{3,7},{5,1},{7,3},{8,12},{10,14},{12... | collective-permute-start | bytes 392 | tf_op jit(solution)/shard_map/ppermute | solution.py:333
  9.9 5.8 %collective-permute-start.2 = (s32[4,8]{1,0:T(4,128)}, s32[4,8]{1,0:T(4,128)S(1)}, u32[]{:S(2)}, u32[]{:S(2)}) collective-permute-start(s32[4,8]{1,0:T(4,128)} %source_ref.1), channel_id=1, source_target_pairs={{0,6},{2,4},{4,2},{6,0},{1,7},{3,5},{5,3},{7,1},{8,14},{10,12},{12... | collective-permute-start | bytes 392 | tf_op jit(solution)/shard_map/ppermute | solution.py:333
  15.7 1.2 %copy-start.2 = (bf16[512,1024]{1,0:T(8,128)(2,1)S(1)}, bf16[512,1024]{1,0:T(8,128)(2,1)}, u32[]{:S(2)}) copy-start(bf16[512,1024]{1,0:T(8,128)(2,1)} %density_ref.3) | copy-start | bytes 3145732
  16.9 0.7 copy-start.5
  18.9 3.3 %copy-start = (bf16[2048,2048]{1,0:T(8,128)(2,1)}, bf16[2048,2048]{1,0:T(8,128)(2,1)S(1)}, u32[]{:S(2)}) copy-start(bf16[2048,2048]{1,0:T(8,128)(2,1)S(1)} %get-tuple-element.18.refs_16_) | copy-start | bytes 25165828
  22.2 8.1 %collective-permute-start.11 = (bf16[128,1024]{1,0:T(8,128)(2,1)S(1)}, bf16[128,1024]{1,0:T(8,128)(2,1)S(1)}, u32[]{:S(2)}, u32[]{:S(2)}) collective-permute-start(bf16[128,1024]{1,0:T(8,128)(2,1)S(1)} %get-tuple-element.16), channel_id=1, source_target_pairs={{0,2},{2,0},{4,6},{6,4},{1,3},{3,1},{5,7},{7,5},{8,10},{10,8},{12,... | collective-permute-start | bytes 786440 | tf_op jit(solution)/shard_map/ppermute | solution.py:333
  22.8 7.5 %collective-permute-start.6 = (bf16[128,1024]{1,0:T(8,128)(2,1)S(1)}, bf16[128,1024]{1,0:T(8,128)(2,1)S(1)}, u32[]{:S(2)}, u32[]{:S(2)}) collective-permute-start(bf16[128,1024]{1,0:T(8,128)(2,1)S(1)} %collective-permute-done.5.refs_2_), channel_id=1, source_target_pairs={{2,4},{4,2},{3,5},{5,3},{10,12},{12,10},{11,13},{13,11},{18,20},{2... | collective-permute-start | bytes 786440 | tf_op jit(solution)/shard_map/ppermute | solution.py:333
  23.4 11.2 %collective-permute-start.13 = (bf16[128,1024]{1,0:T(8,128)(2,1)S(1)}, bf16[128,1024]{1,0:T(8,128)(2,1)S(1)}, u32[]{:S(2)}, u32[]{:S(2)}) collective-permute-start(bf16[128,1024]{1,0:T(8,128)(2,1)S(1)} %collective-permute-done.4), channel_id=1, source_target_pairs={{2,0},{4,6},{3,1},{5,7},{10,8},{12,14},{11,9},{13,15},{18,16},{20,... | collective-permute-start | bytes 786440 | tf_op jit(solution)/shard_map/ppermute | solution.py:333
  24.8 11.5 %collective-permute-start.22 = (bf16[128,1024]{1,0:T(8,128)(2,1)S(1)}, bf16[128,1024]{1,0:T(8,128)(2,1)S(1)}, u32[]{:S(2)}, u32[]{:S(2)}) collective-permute-start(bf16[128,1024]{1,0:T(8,128)(2,1)S(1)} %collective-permute-done.5.refs_2_), channel_id=1, source_target_pairs={{0,8},{1,17},{8,0},{9,25},{16,24},{17,1},{24,16},{25,9},{2,10},{3,... | collective-permute-start | bytes 786440 | tf_op jit(solution)/shard_map/ppermute | solution.py:341
  26.3 11.4 %collective-permute-start.24 = (bf16[128,1024]{1,0:T(8,128)(2,1)S(1)}, bf16[128,1024]{1,0:T(8,128)(2,1)S(1)}, u32[]{:S(2)}, u32[]{:S(2)}) collective-permute-start(bf16[128,1024]{1,0:T(8,128)(2,1)S(1)} %collective-permute-done.5.refs_2_), channel_id=1, source_target_pairs={{0,16},{1,9},{8,24},{9,1},{16,0},{17,25},{24,8},{25,17},{2,18},{3,... | collective-permute-start | bytes 786440 | tf_op jit(solution)/shard_map/ppermute | solution.py:341
  30.2 7.5 %collective-permute-start.21 = (bf16[128,1024]{1,0:T(8,128)(2,1)S(1)}, bf16[128,1024]{1,0:T(8,128)(2,1)S(1)}, u32[]{:S(2)}, u32[]{:S(2)}) collective-permute-start(bf16[128,1024]{1,0:T(8,128)(2,1)S(1)} %collective-permute-done.5.refs_2_), channel_id=1, source_target_pairs={{0,1},{1,0},{2,3},{3,2},{4,5},{5,4},{6,7},{7,6},{8,9},{9,8},{10,11... | collective-permute-start | bytes 786440 | tf_op jit(solution)/shard_map/ppermute | solution.py:333
  30.2 8.8 %collective-permute-start.12 = (bf16[128,1024]{1,0:T(8,128)(2,1)S(1)}, bf16[128,1024]{1,0:T(8,128)(2,1)S(1)}, u32[]{:S(2)}, u32[]{:S(2)}) collective-permute-start(bf16[128,1024]{1,0:T(8,128)(2,1)S(1)} %collective-permute-done.11.refs_0_), channel_id=1, source_target_pairs={{0,1},{1,0},{2,3},{3,2},{4,5},{5,4},{6,7},{7,6},{8,9},{9,8},{10,11... | collective-permute-start | bytes 786440 | tf_op jit(solution)/shard_map/ppermute | solution.py:333
  34.7 8.0 %collective-permute-start.14 = (bf16[128,1024]{1,0:T(8,128)(2,1)S(1)}, bf16[128,1024]{1,0:T(8,128)(2,1)S(1)}, u32[]{:S(2)}, u32[]{:S(2)}) collective-permute-start(bf16[128,1024]{1,0:T(8,128)(2,1)S(1)} %broadcast_select_fusion.refs_8_), channel_id=1, source_target_pairs={{0,8},{1,17},{8,0},{9,25},{16,24},{17,1},{24,16},{25,9},{2,10},{3,... | collective-permute-start | bytes 786440 | tf_op jit(solution)/shard_map/ppermute | solution.py:341
  36.2 6.4 %collective-permute-start.28 = (bf16[128,1024]{1,0:T(8,128)(2,1)S(1)}, bf16[128,1024]{1,0:T(8,128)(2,1)S(1)}, u32[]{:S(2)}, u32[]{:S(2)}) collective-permute-start(bf16[128,1024]{1,0:T(8,128)(2,1)S(1)} %broadcast_select_fusion.refs_8_), channel_id=1, source_target_pairs={{0,16},{1,9},{8,24},{9,1},{16,0},{17,25},{24,8},{25,17},{2,18},{3,... | collective-permute-start | bytes 786440 | tf_op jit(solution)/shard_map/ppermute | solution.py:341
  37.7 5.4 %collective-permute-start.26 = (bf16[128,1024]{1,0:T(8,128)(2,1)S(1)}, bf16[128,1024]{1,0:T(8,128)(2,1)S(1)}, u32[]{:S(2)}, u32[]{:S(2)}) collective-permute-start(bf16[128,1024]{1,0:T(8,128)(2,1)S(1)} %broadcast_select_fusion.refs_8_), channel_id=1, source_target_pairs={{0,1},{1,0},{2,3},{3,2},{4,5},{5,4},{6,7},{7,6},{8,9},{9,8},{10,11... | collective-permute-start | bytes 786440 | tf_op jit(solution)/shard_map/ppermute | solution.py:333
  37.7 10.6 %collective-permute-start.7 = (bf16[128,1024]{1,0:T(8,128)(2,1)S(1)}, bf16[128,1024]{1,0:T(8,128)(2,1)S(1)}, u32[]{:S(2)}, u32[]{:S(2)}) collective-permute-start(bf16[128,1024]{1,0:T(8,128)(2,1)S(1)} %collective-permute-done.6), channel_id=1, source_target_pairs={{2,0},{4,6},{3,1},{5,7},{10,8},{12,14},{11,9},{13,15},{18,16},{20,... | collective-permute-start | bytes 786440 | tf_op jit(solution)/shard_map/ppermute | solution.py:333
  39.0 24.9 %collective-permute-start.20 = (bf16[512,1024]{1,0:T(8,128)(2,1)S(1)}, bf16[512,1024]{1,0:T(8,128)(2,1)S(1)}, u32[]{:S(2)}, u32[]{:S(2)}) collective-permute-start(bf16[512,1024]{1,0:T(8,128)(2,1)S(1)} %get-tuple-element.17), channel_id=1, source_target_pairs={{0,1},{1,0},{2,3},{3,2},{4,5},{5,4},{6,7},{7,6},{8,9},{9,8},{10,11... | collective-permute-start | bytes 3145736 | tf_op jit(solution)/shard_map/ppermute | solution.py:333
  42.6 5.7 %collective-permute-start.23 = (bf16[128,1024]{1,0:T(8,128)(2,1)S(1)}, bf16[128,1024]{1,0:T(8,128)(2,1)S(1)}, u32[]{:S(2)}, u32[]{:S(2)}) collective-permute-start(bf16[128,1024]{1,0:T(8,128)(2,1)S(1)} %collective-permute-done.22.refs_4_), channel_id=1, source_target_pairs={{0,1},{1,0},{2,3},{3,2},{4,5},{5,4},{6,7},{7,6},{8,9},{9,8},{10,11... | collective-permute-start | bytes 786440 | tf_op jit(solution)/shard_map/ppermute | solution.py:333
  42.7 6.3 %collective-permute-start.25 = (bf16[128,1024]{1,0:T(8,128)(2,1)S(1)}, bf16[128,1024]{1,0:T(8,128)(2,1)S(1)}, u32[]{:S(2)}, u32[]{:S(2)}) collective-permute-start(bf16[128,1024]{1,0:T(8,128)(2,1)S(1)} %collective-permute-done.24.refs_6_), channel_id=1, source_target_pairs={{0,1},{1,0},{2,3},{3,2},{4,5},{5,4},{6,7},{7,6},{8,9},{9,8},{10,11... | collective-permute-start | bytes 786440 | tf_op jit(solution)/shard_map/ppermute | solution.py:333
  43.2 6.0 %collective-permute-start.27 = (bf16[128,1024]{1,0:T(8,128)(2,1)S(1)}, bf16[128,1024]{1,0:T(8,128)(2,1)S(1)}, u32[]{:S(2)}, u32[]{:S(2)}) collective-permute-start(bf16[128,1024]{1,0:T(8,128)(2,1)S(1)} %collective-permute-done.14.refs_10_), channel_id=1, source_target_pairs={{0,1},{1,0},{2,3},{3,2},{4,5},{5,4},{6,7},{7,6},{8,9},{9,8},{10,11... | collective-permute-start | bytes 786440 | tf_op jit(solution)/shard_map/ppermute | solution.py:333
  48.3 2.4 %collective-permute-start.29 = (bf16[128,1024]{1,0:T(8,128)(2,1)S(1)}, bf16[128,1024]{1,0:T(8,128)(2,1)S(1)}, u32[]{:S(2)}, u32[]{:S(2)}) collective-permute-start(bf16[128,1024]{1,0:T(8,128)(2,1)S(1)} %collective-permute-done.28.refs_12_), channel_id=1, source_target_pairs={{0,1},{1,0},{2,3},{3,2},{4,5},{5,4},{6,7},{7,6},{8,9},{9,8},{10,11... | collective-permute-start | bytes 786440 | tf_op jit(solution)/shard_map/ppermute | solution.py:333
  48.4 9.1 %collective-permute-start.8 = (bf16[128,1024]{1,0:T(8,128)(2,1)S(1)}, bf16[128,1024]{1,0:T(8,128)(2,1)S(1)}, u32[]{:S(2)}, u32[]{:S(2)}) collective-permute-start(bf16[128,1024]{1,0:T(8,128)(2,1)S(1)} %broadcast_select_fusion.1.refs_14_), channel_id=1, source_target_pairs={{0,8},{1,17},{8,0},{9,25},{16,24},{17,1},{24,16},{25,9},{2,10},{3,... | collective-permute-start | bytes 786440 | tf_op jit(solution)/shard_map/ppermute | solution.py:341
  49.0 8.5 %collective-permute-start.30 = (bf16[128,1024]{1,0:T(8,128)(2,1)S(1)}, bf16[128,1024]{1,0:T(8,128)(2,1)S(1)}, u32[]{:S(2)}, u32[]{:S(2)}) collective-permute-start(bf16[128,1024]{1,0:T(8,128)(2,1)S(1)} %broadcast_select_fusion.1.refs_14_), channel_id=1, source_target_pairs={{0,1},{1,0},{2,3},{3,2},{4,5},{5,4},{6,7},{7,6},{8,9},{9,8},{10,11... | collective-permute-start | bytes 786440 | tf_op jit(solution)/shard_map/ppermute | solution.py:333
  49.2 8.3 %collective-permute-start.15 = (bf16[128,1024]{1,0:T(8,128)(2,1)S(1)}, bf16[128,1024]{1,0:T(8,128)(2,1)S(1)}, u32[]{:S(2)}, u32[]{:S(2)}) collective-permute-start(bf16[128,1024]{1,0:T(8,128)(2,1)S(1)} %collective-permute-done.14.refs_10_), channel_id=1, source_target_pairs={{0,16},{1,9},{8,24},{9,1},{16,0},{17,25},{24,8},{25,17},{2,18},{3,... | collective-permute-start | bytes 786440 | tf_op jit(solution)/shard_map/ppermute | solution.py:341
  50.7 9.3 %collective-permute-start.18 = (bf16[128,1024]{1,0:T(8,128)(2,1)S(1)}, bf16[128,1024]{1,0:T(8,128)(2,1)S(1)}, u32[]{:S(2)}, u32[]{:S(2)}) collective-permute-start(bf16[128,1024]{1,0:T(8,128)(2,1)S(1)} %broadcast_select_fusion.1.refs_14_), channel_id=1, source_target_pairs={{0,16},{1,9},{8,24},{9,1},{16,0},{17,25},{24,8},{25,17},{2,18},{3,... | collective-permute-start | bytes 786440 | tf_op jit(solution)/shard_map/ppermute | solution.py:341
  57.5 6.4 %collective-permute-start.9 = (bf16[128,1024]{1,0:T(8,128)(2,1)S(1)}, bf16[128,1024]{1,0:T(8,128)(2,1)S(1)}, u32[]{:S(2)}, u32[]{:S(2)}) collective-permute-start(bf16[128,1024]{1,0:T(8,128)(2,1)S(1)} %collective-permute-done.8.refs_4_), channel_id=1, source_target_pairs={{0,16},{1,9},{8,24},{9,1},{16,0},{17,25},{24,8},{25,17},{2,18},{3,... | collective-permute-start | bytes 786440 | tf_op jit(solution)/shard_map/ppermute | solution.py:341
  57.5 14.6 %collective-permute-start.17 = (bf16[128,1024]{1,0:T(8,128)(2,1)S(1)}, bf16[128,1024]{1,0:T(8,128)(2,1)S(1)}, u32[]{:S(2)}, u32[]{:S(2)}) collective-permute-start(bf16[128,1024]{1,0:T(8,128)(2,1)S(1)} %collective-permute-done.8.refs_4_), channel_id=1, source_target_pairs={{0,1},{1,0},{2,3},{3,2},{4,5},{5,4},{6,7},{7,6},{8,9},{9,8},{10,11... | collective-permute-start | bytes 786440 | tf_op jit(solution)/shard_map/ppermute | solution.py:333
  57.6 14.5 %collective-permute-start.16 = (bf16[128,1024]{1,0:T(8,128)(2,1)S(1)}, bf16[128,1024]{1,0:T(8,128)(2,1)S(1)}, u32[]{:S(2)}, u32[]{:S(2)}) collective-permute-start(bf16[128,1024]{1,0:T(8,128)(2,1)S(1)} %collective-permute-done.15.refs_2_), channel_id=1, source_target_pairs={{0,1},{1,0},{2,3},{3,2},{4,5},{5,4},{6,7},{7,6},{8,9},{9,8},{10,11... | collective-permute-start | bytes 786440 | tf_op jit(solution)/shard_map/ppermute | solution.py:333
  60.0 12.1 %collective-permute-start.19 = (bf16[128,1024]{1,0:T(8,128)(2,1)S(1)}, bf16[128,1024]{1,0:T(8,128)(2,1)S(1)}, u32[]{:S(2)}, u32[]{:S(2)}) collective-permute-start(bf16[128,1024]{1,0:T(8,128)(2,1)S(1)} %collective-permute-done.18.refs_6_), channel_id=1, source_target_pairs={{0,1},{1,0},{2,3},{3,2},{4,5},{5,4},{6,7},{7,6},{8,9},{9,8},{10,11... | collective-permute-start | bytes 786440 | tf_op jit(solution)/shard_map/ppermute | solution.py:333
  63.9 11.0 %collective-permute-start.10 = (bf16[128,1024]{1,0:T(8,128)(2,1)S(1)}, bf16[128,1024]{1,0:T(8,128)(2,1)S(1)}, u32[]{:S(2)}, u32[]{:S(2)}) collective-permute-start(bf16[128,1024]{1,0:T(8,128)(2,1)S(1)} %collective-permute-done.9.refs_5_), channel_id=1, source_target_pairs={{0,1},{1,0},{2,3},{3,2},{4,5},{5,4},{6,7},{7,6},{8,9},{9,8},{10,11... | collective-permute-start | bytes 786440 | tf_op jit(solution)/shard_map/ppermute | solution.py:333
  63.9 11.0 %collective-permute-start.3 = (s32[4,4,8]{2,1,0:T(4,128)S(1)}, s32[4,4,8]{2,1,0:T(4,128)S(1)}, u32[]{:S(2)}, u32[]{:S(2)}) collective-permute-start(s32[4,4,8]{2,1,0:T(4,128)S(1)} %get-tuple-element.15.refs_3_), channel_id=1, source_target_pairs={{0,1},{1,0},{2,3},{3,2},{4,5},{5,4},{6,7},{7,6},{8,9},{9,8},{10,11... | collective-permute-start | bytes 1544 | tf_op jit(solution)/shard_map/ppermute | solution.py:333
  64.4 3.4 %copy-start.1 = (bf16[2048,2048]{1,0:T(8,128)(2,1)S(1)}, bf16[2048,2048]{1,0:T(8,128)(2,1)}, u32[]{:S(2)}) copy-start(bf16[2048,2048]{1,0:T(8,128)(2,1)} %copy-done) | copy-start | bytes 25165828
  67.8 0.9 %copy-start.4 = (bf16[128,1024]{1,0:T(8,128)(2,1)S(1)}, bf16[128,1024]{1,0:T(8,128)(2,1)}, u32[]{:S(2)}) copy-start(bf16[128,1024]{1,0:T(8,128)(2,1)} %unit.1.refs_0_) | copy-start | bytes 786436
  72.1 2.8 %copy-start.3 = (bf16[32,3,128,128]{3,2,1,0:T(8,128)(2,1)S(1)}, bf16[32,3,128,128]{3,2,1,0:T(8,128)(2,1)}, u32[]{:S(2)}) copy-start(bf16[32,3,128,128]{3,2,1,0:T(8,128)(2,1)} %refs_10_.1) | copy-start | bytes 9437188
  72.1 2.8 %copy-start.6 = (s32[32,1]{0,1:T(1,128)S(1)}, s32[32,1]{0,1:T(1,128)}, u32[]{:S(2)}) copy-start(s32[32,1]{0,1:T(1,128)} %param.8) | copy-start | bytes 388
  72.1 2.8 %copy-start.7 = (s32[32]{0:T(128)S(1)}, s32[32]{0:T(128)}, u32[]{:S(2)}) copy-start(s32[32]{0:T(128)} %refs_1_.1) | copy-start | bytes 388
  72.1 2.8 %copy-start.8 = (s32[32]{0:T(128)S(1)}, s32[32]{0:T(128)}, u32[]{:S(2)}) copy-start(s32[32]{0:T(128)} %refs_2_.1) | copy-start | bytes 388
where the time goes:
time: 82.5 us; the launch traced here: 82.1 us
  waiting for transfers between devices  29.7 us (36%)
  starting transfers between devices  26.4 us (32%)
  Pallas kernels  16.2 us (20%)
  local copies, waits for them, and re-layouts  9.54 us (12%)
    ppermute x23, starting transfers between devices, send(): return lax.ppermute(value, axis, pairs)  17.6 us
    ppermute x8, waiting for transfers between devices, spread(): return lax.ppermute(value, ('layer', 'col'), pairs)  14.9 us
    ppermute x23, waiting for transfers between devices, send(): return lax.ppermute(value, axis, pairs)  14.8 us
    unnamed x18, local copies, waits for them, and re-layouts  9.54 us
    ppermute x8, starting transfers between devices, spread(): return lax.ppermute(value, ('layer', 'col'), pairs)  8.75 us
    pallas_call x1, Pallas kernels, resident_step(): pl.pallas_call(functools.partial(force_kernel, tuple((u[:2] for u in late...  7.16 us
    pallas_call x2, Pallas kernels, add_squares(): pl.pallas_call(functools.partial(square_kernel, layout, pairs, zeros, sha...  6.08 us
    pallas_call x1, Pallas kernels, resident_step(): pl.pallas_call(functools.partial(unit_kernel, share), out_shape=unit_shap...  1.72 us
  transfers between devices with their start and end apart: 31, of which 8 were waited for; matrix products, arithmetic and copies ran while one was open for 0% of the time, Pallas kernels for 9%

commit v1 on v0

--- a/solution.py
+++ b/solution.py
@@ -12,6 +12,7 @@
 ATOM_DEV = 8
 RESIDENT_GRID = (4, 4, 2)
 ALONG_X, ALONG_Y = 1, 2
+UNROLL = 8
 
 
 def block_filter(matrix, kept_blocks):
@@ -190,20 +191,25 @@
     rows = share * BS
     width = col_blocks * BS
     copies = []
-    for slot, (ref, (unit, half, placed)) in enumerate(zip(unit_refs, layout)):
+    for slot, (ref, (unit, half)) in enumerate(zip(unit_refs, layout)):
         core = grid_col ^ half
         columns = pl.ds(pl.multiple_of(core * width, width), width)
-        if not placed:
-            height = ref.shape[0]
-            start = unit_start(layer_id, grid_row, core, unit, row_blocks, rows)
-            start = pl.multiple_of(start, height)
-            begin(copies, ref, full.at[pl.ds(start, height), columns], sems.at[slot])
+        height = ref.shape[0]
+        start = unit_start(layer_id, grid_row, core, unit, row_blocks, rows)
+        start = pl.multiple_of(start, height)
+        begin(copies, ref, full.at[pl.ds(start, height), columns], sems.at[slot])
         if first and not unit[1]:
             source = ref
             if unit[1] is None:
                 source = ref.at[pl.ds(pl.multiple_of(layer_id * rows, rows), rows), :]
             start = pl.multiple_of((grid_row ^ unit[0]) * rows, rows)
             begin(copies, source, left.at[pl.ds(start, rows), columns], left_sems.at[slot])
+    if first:
+        start = unit_start(layer_id, grid_row, grid_col, (0, 0), row_blocks, rows)
+        columns = pl.ds(pl.multiple_of(grid_col * width, width), width)
+        source = full.at[pl.ds(pl.multiple_of(start, rows), rows), columns]
+        start = pl.multiple_of(grid_row * rows, rows)
+        begin(copies, source, left.at[pl.ds(start, rows), columns], left_sems.at[count])
     for unit in absent:
         start = unit_start(layer_id, grid_row, grid_col, unit, row_blocks, rows)
         full[pl.ds(pl.multiple_of(start, rows), rows), :] = jnp.zeros(
@@ -221,7 +227,7 @@
     partial[...] = total
 
 
-def force_kernel(late, absent, n_rows, n_cols, share, row_blocks, col_blocks, *refs):
+def force_kernel(late, absent, n_cols, share, row_blocks, col_blocks, *refs):
     tables, refs = refs[:5], refs[5:]
     late_refs, refs = refs[: len(late)], refs[len(late) :]
     (
@@ -236,7 +242,6 @@
         last,
         last_left,
         totals,
-        kept,
         holder_ref,
         slot_ref,
         atom_ref,
@@ -258,7 +263,6 @@
     table_copies = []
     for k, (table, place) in enumerate(zip(tables, places)):
         begin(table_copies, table, place, table_sems.at[k])
-    totals[...] = jnp.zeros_like(totals)
     starts = [
         pl.multiple_of(unit_start(layer_id, grid_row, grid_col, unit, row_blocks, rows), rows)
         for unit in absent
@@ -273,37 +277,33 @@
     square[...] = (partial[...] + more).astype(square.dtype)
     cube = jnp.dot(square[...], full[...], preferred_element_type=jnp.float32)
     purified[...] = (3.0 * square[...].astype(jnp.float32) - 2.0 * cube).astype(purified.dtype)
-
     for copy in table_copies:
         copy.wait()
-    for half in range(2):
-        for d in range(n_rows):
-            pattern_ref = patterns_ref.at[half, d]
-            place, column = grid_row ^ d, grid_col ^ half
-            for i in range(share):
-                for q in range(col_blocks):
-                    value = kept_block(pattern_ref, layer_id * share + i, q, place, column)
-                    kept[place * share + i, column * col_blocks + q] = value.astype(jnp.int32)
-
-    @pl.loop(0, held.shape[0], unroll=4)
+    components = held.shape[1]
+
+    totals[...] = jnp.zeros_like(totals)
+
+    @pl.loop(0, held.shape[0], unroll=UNROLL)
     def _(e):
         h = holder_ref[e]
         s = slot_ref[e]
-        row = (h // n_cols) * share + s // col_blocks
-        column = (h % n_cols) * col_blocks + s % col_blocks
-        block = purified[
-            pl.ds(pl.multiple_of(row * BS, BS), BS), pl.ds(pl.multiple_of(column * BS, BS), BS)
-        ].astype(jnp.float32)
-
-        keep = kept[row, column] == 1
-        for x in range(held.shape[1]):
+        place, core = h // n_cols, h % n_cols
+        row, column = s // col_blocks, s % col_blocks
+        tile_row = layer_id * share + row
+        pattern = patterns_ref[core ^ grid_col, place ^ grid_row, tile_row, column]
+        across = core * col_blocks + column
+        keep = (pattern == 1) | (place * row_blocks + tile_row == across)
+        rows_at = pl.ds(pl.multiple_of((place * share + row) * BS, BS), BS)
+        columns_at = pl.ds(pl.multiple_of(across * BS, BS), BS)
+        block = purified[rows_at, columns_at].astype(jnp.float32)
+        atom = atom_ref[e]
+        for x in range(components):
             product = block * held[e, x].astype(jnp.float32)
             part = jnp.sum(product.reshape(BS // 8, 8, BS), axis=0)
             part = jnp.where(keep, part, jnp.zeros_like(part))
-            totals[x, atom_ref[e]] = totals[x, atom_ref[e]] + part
-
-    sums = jnp.sum(jnp.sum(totals[...], axis=3), axis=2)
-    forces_ref[...] = -2.0 * sums
+            totals[x, atom] = totals[x, atom] + part
+
+    forces_ref[...] = -2.0 * jnp.sum(jnp.sum(totals[...], axis=3), axis=2)
 
 
 VMEM = pl.BlockSpec(memory_space=pltpu.VMEM)
@@ -380,7 +380,7 @@
 
     diagonal = ALONG_X ^ ALONG_Y
     absent = ((3, diagonal),)
-    placed = [((0, 0), 0, True, near), ((0, None), 1, False, other)]
+    placed = [((0, None), 1, other)]
     late = []
     for k, z in ((1, z1), (2, z2), (3, z3)):
         a_ = spread(z, "a")
@@ -392,22 +392,22 @@
                 if (k, kind) in absent:
                     late.append(((k, kind), half, part))
                 else:
-                    placed.append(((k, kind), half, False, part))
+                    placed.append(((k, kind), half, part))
     left_shape = jax.ShapeDtypeStruct((tall, width), dtype)
     partial_shape = jax.ShapeDtypeStruct((tall, width), jnp.float32)
 
     def add_squares(units, pairs, zeros, full, *held):
         count = len(units)
-        layout = tuple(u[:3] for u in units)
+        layout = tuple(u[:2] for u in units)
         return pl.pallas_call(
             functools.partial(square_kernel, layout, pairs, zeros, share, row_blocks, col_blocks),
             out_shape=[full_shape] + ([] if held else [left_shape]) + [partial_shape],
             in_specs=[HBM] * count + [VMEM] * (1 + len(held)),
             out_specs=[VMEM] * (2 if held else 3),
             input_output_aliases={count: 0, count + 1: 1} if held else {count: 0},
-            scratch_shapes=[pltpu.SemaphoreType.DMA((count,))] * 2,
+            scratch_shapes=[pltpu.SemaphoreType.DMA((count + 1,))] * 2,
             compiler_params=pltpu.CompilerParams(vmem_limit_bytes=24 * 2**20),
-        )(*[u[3] for u in units], full, *held)
+        )(*[u[2] for u in units], full, *held)
 
     behind = ((1, diagonal), (2, diagonal), (3, "a"), (3, "b"))
     early = [u for u in placed if u[0] not in behind]
@@ -421,14 +421,7 @@
     components = derivative.shape[1]
     return pl.pallas_call(
         functools.partial(
-            force_kernel,
-            tuple(u[:2] for u in late),
-            absent,
-            n_rows,
-            n_cols,
-            share,
-            row_blocks,
-            col_blocks,
+            force_kernel, tuple(u[:2] for u in late), absent, n_cols, share, row_blocks, col_blocks
         ),
         out_shape=[jax.ShapeDtypeStruct((components, ATOM_DEV), jnp.float32), full_shape],
         in_specs=[ANY] * len(tables) + [HBM] * n_late + [VMEM] * 4,
@@ -440,7 +433,6 @@
             pltpu.VMEM((len(absent) * rows, width), dtype),
             pltpu.VMEM((tall, len(absent) * rows), dtype),
             pltpu.VMEM((components, ATOM_DEV, 8, BS), jnp.float32),
-            pltpu.SMEM((n_rows * share, n_cols * col_blocks), jnp.int32),
             pltpu.SMEM(slot_index.shape, jnp.int32),
             pltpu.SMEM(slot_index.shape, jnp.int32),
             pltpu.SMEM(slot_index.shape, jnp.int32),

time: 82.5 us -> 81.5 us (0.988)
  local copies, waits for them, and re-layouts: 9.54 us -> 8.59 us
    unnamed x18 -> x16, local copies, waits for them, and re-layouts: 9.54 us -> 8.59 us
where the time goes in v1:
time: 81.5 us; the launch traced here: 81.2 us
  waiting for transfers between devices  29.7 us (36%)
  starting transfers between devices  26.4 us (32%)
  Pallas kernels  16.3 us (20%)
  local copies, waits for them, and re-layouts  8.59 us (11%)
    ppermute x23, starting transfers between devices, send(): return lax.ppermute(value, axis, pairs)  17.6 us
    ppermute x8, waiting for transfers between devices, spread(): return lax.ppermute(value, ('layer', 'col'), pairs)  14.9 us
    ppermute x23, waiting for transfers between devices, send(): return lax.ppermute(value, axis, pairs)  14.8 us
    ppermute x8, starting transfers between devices, spread(): return lax.ppermute(value, ('layer', 'col'), pairs)  8.75 us
    unnamed x16, local copies, waits for them, and re-layouts  8.59 us
    pallas_call x1, Pallas kernels, resident_step(): pl.pallas_call(functools.partial(force_kernel, tuple((u[:2] for u in late...  7.04 us
    pallas_call x2, Pallas kernels, add_squares(): pl.pallas_call(functools.partial(square_kernel, layout, pairs, zeros, sha...  6.25 us
    pallas_call x1, Pallas kernels, resident_step(): pl.pallas_call(functools.partial(unit_kernel, share), out_shape=unit_shap...  1.72 us
  transfers between devices with their start and end apart: 31, of which 8 were waited for; matrix products, arithmetic and copies ran while one was open for 0% of the time, Pallas kernels for 9%

profile of v1, /device:TPU:0, one launch (start us, length us, event | category | flops | bytes accessed | tf_op | source)
XLA Modules:
  0.0 81.2 jit_solution(11249476156288777036)
XLA Ops:
  0.0 1.7 %unit.1 = bf16[128,1024]{1,0:T(8,128)(2,1)} custom-call(bf16[512,1024]{1,0:T(8,128)(2,1)} %density_ref.3, s32[4,8]{1,0:T(4,128)} %source_ref.1), custom_call_target="tpu_custom_call" | custom-call | tf_op jit(solution)/shard_map/unit/pallas_call | solution.py:346
  1.7 3.1 %collective-permute-start.5 = (bf16[128,1024]{1,0:T(8,128)(2,1)}, bf16[128,1024]{1,0:T(8,128)(2,1)S(1)}, u32[]{:S(2)}, u32[]{:S(2)}) collective-permute-start(bf16[128,1024]{1,0:T(8,128)(2,1)} %unit.1), channel_id=1, source_target_pairs={{0,2},{2,0},{4,6},{6,4},{1,3},{3,1},{5,7},{7,5},{8,10},{10,8},{12,... | collective-permute-start | bytes 786440 | tf_op jit(solution)/shard_map/ppermute | solution.py:333
  4.9 0.7 collective-permute-start.4
  5.5 4.4 %collective-permute-start = (s32[4,8]{1,0:T(4,128)}, s32[4,8]{1,0:T(4,128)S(1)}, u32[]{:S(2)}, u32[]{:S(2)}) collective-permute-start(s32[4,8]{1,0:T(4,128)} %source_ref.1), channel_id=1, source_target_pairs={{0,2},{2,0},{4,6},{6,4},{1,3},{3,1},{5,7},{7,5},{8,10},{10,8},{12,... | collective-permute-start | bytes 392 | tf_op jit(solution)/shard_map/ppermute | solution.py:333
  9.9 0.0 collective-permute-start.1
  9.9 2.4 %collective-permute-start.2 = (s32[4,8]{1,0:T(4,128)}, s32[4,8]{1,0:T(4,128)S(1)}, u32[]{:S(2)}, u32[]{:S(2)}) collective-permute-start(s32[4,8]{1,0:T(4,128)} %source_ref.1), channel_id=1, source_target_pairs={{0,6},{2,4},{4,2},{6,0},{1,7},{3,5},{5,3},{7,1},{8,14},{10,12},{12... | collective-permute-start | bytes 392 | tf_op jit(solution)/shard_map/ppermute | solution.py:333
  12.4 0.0 collective-permute-done.refs_1_
  12.4 3.3 %collective-permute-done.1.refs_2_ = s32[4,8]{1,0:T(4,128)S(1)} collective-permute-done((s32[4,8]{1,0:T(4,128)}, s32[4,8]{1,0:T(4,128)S(1)}, u32[]{:S(2)}, u32[]{:S(2)}) %collective-permute-start.1) | collective-permute-done | bytes 160 | tf_op jit(solution)/shard_map/ppermute | solution.py:333
  15.7 0.0 collective-permute-done.2.refs_3_
  15.7 1.2 %copy-done.2 = bf16[512,1024]{1,0:T(8,128)(2,1)S(1)} copy-done((bf16[512,1024]{1,0:T(8,128)(2,1)S(1)}, bf16[512,1024]{1,0:T(8,128)(2,1)}, u32[]{:S(2)}) %copy-start.2) | copy-done | bytes 1048600
  16.9 0.7 copy-done.4
  17.6 1.3 %filter.1 = (bf16[512,1024]{1,0:T(8,128)(2,1)S(1)}, bf16[128,1024]{1,0:T(8,128)(2,1)S(1)}, bf16[2048,2048]{1,0:T(8,128)(2,1)S(1)}, s32[4,4,8]{2,1,0:T(4,128)S(1)}) custom-call(bf16[512,1024]{1,0:T(8,128)(2,1)S(1)} %copy-done.2, s32[4,8]{1,0:T(4,128)S(1)} %copy-done.4, s32[4,8]{1,0:T(4,128)S(1)} %collective-permute-done.refs_1_, ...), custom_call_target="tpu_custom_call" | custom-call | tf_op jit(solution)/shard_map/filter/pallas_call | solution.py:369
  18.9 3.3 %copy-done = bf16[2048,2048]{1,0:T(8,128)(2,1)} copy-done((bf16[2048,2048]{1,0:T(8,128)(2,1)}, bf16[2048,2048]{1,0:T(8,128)(2,1)S(1)}, u32[]{:S(2)}) %copy-start) | copy-done | bytes 8388632
  22.2 0.6 collective-permute-start.11
  22.8 0.0 collective-permute-done.5.refs_1_
  22.8 0.7 collective-permute-start.6
  23.4 0.0 collective-permute-done.4
  23.4 1.3 %collective-permute-start.13 = (bf16[128,1024]{1,0:T(8,128)(2,1)S(1)}, bf16[128,1024]{1,0:T(8,128)(2,1)S(1)}, u32[]{:S(2)}, u32[]{:S(2)}) collective-permute-start(bf16[128,1024]{1,0:T(8,128)(2,1)S(1)} %collective-permute-done.4), channel_id=1, source_target_pairs={{2,0},{4,6},{3,1},{5,7},{10,8},{12,14},{11,9},{13,15},{18,16},{20,... | collective-permute-start | bytes 786440 | tf_op jit(solution)/shard_map/ppermute | solution.py:333
  24.8 1.5 %collective-permute-start.22 = (bf16[128,1024]{1,0:T(8,128)(2,1)S(1)}, bf16[128,1024]{1,0:T(8,128)(2,1)S(1)}, u32[]{:S(2)}, u32[]{:S(2)}) collective-permute-start(bf16[128,1024]{1,0:T(8,128)(2,1)S(1)} %collective-permute-done.5.refs_1_), channel_id=1, source_target_pairs={{0,8},{1,17},{8,0},{9,25},{16,24},{17,1},{24,16},{25,9},{2,10},{3,... | collective-permute-start | bytes 786440 | tf_op jit(solution)/shard_map/ppermute | solution.py:341
  26.3 1.5 %collective-permute-start.24 = (bf16[128,1024]{1,0:T(8,128)(2,1)S(1)}, bf16[128,1024]{1,0:T(8,128)(2,1)S(1)}, u32[]{:S(2)}, u32[]{:S(2)}) collective-permute-start(bf16[128,1024]{1,0:T(8,128)(2,1)S(1)} %collective-permute-done.5.refs_1_), channel_id=1, source_target_pairs={{0,16},{1,9},{8,24},{9,1},{16,0},{17,25},{24,8},{25,17},{2,18},{3,... | collective-permute-start | bytes 786440 | tf_op jit(solution)/shard_map/ppermute | solution.py:341
  27.8 2.4 %collective-permute-done.11.refs_0_ = bf16[128,1024]{1,0:T(8,128)(2,1)S(1)} collective-permute-done((bf16[128,1024]{1,0:T(8,128)(2,1)S(1)}, bf16[128,1024]{1,0:T(8,128)(2,1)S(1)}, u32[]{:S(2)}, u32[]{:S(2)}) %collective-permute-start.11) | collective-permute-done | bytes 262176 | tf_op jit(solution)/shard_map/ppermute | solution.py:333
  30.2 0.0 collective-permute-start.21
  30.2 0.0 collective-permute-done.6
  30.2 0.5 collective-permute-start.12
  30.8 3.9 %collective-permute-done.13 = bf16[128,1024]{1,0:T(8,128)(2,1)S(1)} collective-permute-done((bf16[128,1024]{1,0:T(8,128)(2,1)S(1)}, bf16[128,1024]{1,0:T(8,128)(2,1)S(1)}, u32[]{:S(2)}, u32[]{:S(2)}) %collective-permute-start.13) | collective-permute-done | bytes 262176 | tf_op jit(solution)/shard_map/ppermute | solution.py:333
  34.7 1.5 %collective-permute-start.14 = (bf16[128,1024]{1,0:T(8,128)(2,1)S(1)}, bf16[128,1024]{1,0:T(8,128)(2,1)S(1)}, u32[]{:S(2)}, u32[]{:S(2)}) collective-permute-start(bf16[128,1024]{1,0:T(8,128)(2,1)S(1)} %broadcast_select_fusion.refs_7_), channel_id=1, source_target_pairs={{0,8},{1,17},{8,0},{9,25},{16,24},{17,1},{24,16},{25,9},{2,10},{3,... | collective-permute-start | bytes 786440 | tf_op jit(solution)/shard_map/ppermute | solution.py:341
  36.2 0.0 collective-permute-done.22.refs_3_
  36.2 1.5 %collective-permute-start.28 = (bf16[128,1024]{1,0:T(8,128)(2,1)S(1)}, bf16[128,1024]{1,0:T(8,128)(2,1)S(1)}, u32[]{:S(2)}, u32[]{:S(2)}) collective-permute-start(bf16[128,1024]{1,0:T(8,128)(2,1)S(1)} %broadcast_select_fusion.refs_7_), channel_id=1, source_target_pairs={{0,16},{1,9},{8,24},{9,1},{16,0},{17,25},{24,8},{25,17},{2,18},{3,... | collective-permute-start | bytes 786440 | tf_op jit(solution)/shard_map/ppermute | solution.py:341
  37.7 0.0 collective-permute-done.24.refs_5_
  37.7 0.0 collective-permute-start.26
  37.7 1.3 %collective-permute-start.7 = (bf16[128,1024]{1,0:T(8,128)(2,1)S(1)}, bf16[128,1024]{1,0:T(8,128)(2,1)S(1)}, u32[]{:S(2)}, u32[]{:S(2)}) collective-permute-start(bf16[128,1024]{1,0:T(8,128)(2,1)S(1)} %collective-permute-done.6), channel_id=1, source_target_pairs={{2,0},{4,6},{3,1},{5,7},{10,8},{12,14},{11,9},{13,15},{18,16},{20,... | collective-permute-start | bytes 786440 | tf_op jit(solution)/shard_map/ppermute | solution.py:333
  39.0 0.0 collective-permute-done.12.refs_1_
  39.0 0.6 collective-permute-start.20
  39.6 3.0 %collective-permute-done.14.refs_9_ = bf16[128,1024]{1,0:T(8,128)(2,1)S(1)} collective-permute-done((bf16[128,1024]{1,0:T(8,128)(2,1)S(1)}, bf16[128,1024]{1,0:T(8,128)(2,1)S(1)}, u32[]{:S(2)}, u32[]{:S(2)}) %collective-permute-start.14) | collective-permute-done | bytes 262176 | tf_op jit(solution)/shard_map/ppermute | solution.py:341
  42.7 0.0 collective-permute-start.23
  42.7 0.0 collective-permute-done.28.refs_11_
  42.7 0.5 collective-permute-start.25
  43.2 0.1 collective-permute-start.27
  43.2 5.1 %collective-permute-done.7 = bf16[128,1024]{1,0:T(8,128)(2,1)S(1)} collective-permute-done((bf16[128,1024]{1,0:T(8,128)(2,1)S(1)}, bf16[128,1024]{1,0:T(8,128)(2,1)S(1)}, u32[]{:S(2)}, u32[]{:S(2)}) %collective-permute-start.7) | collective-permute-done | bytes 262176 | tf_op jit(solution)/shard_map/ppermute | solution.py:333
  48.4 0.6 collective-permute-start.8
  49.0 0.2 collective-permute-start.30
  49.2 1.5 %collective-permute-start.15 = (bf16[128,1024]{1,0:T(8,128)(2,1)S(1)}, bf16[128,1024]{1,0:T(8,128)(2,1)S(1)}, u32[]{:S(2)}, u32[]{:S(2)}) collective-permute-start(bf16[128,1024]{1,0:T(8,128)(2,1)S(1)} %collective-permute-done.14.refs_9_), channel_id=1, source_target_pairs={{0,16},{1,9},{8,24},{9,1},{16,0},{17,25},{24,8},{25,17},{2,18},{3,... | collective-permute-start | bytes 786440 | tf_op jit(solution)/shard_map/ppermute | solution.py:341
  50.7 0.5 collective-permute-start.18
  51.2 6.3 %collective-permute-done.8.refs_4_ = bf16[128,1024]{1,0:T(8,128)(2,1)S(1)} collective-permute-done((bf16[128,1024]{1,0:T(8,128)(2,1)S(1)}, bf16[128,1024]{1,0:T(8,128)(2,1)S(1)}, u32[]{:S(2)}, u32[]{:S(2)}) %collective-permute-start.8) | collective-permute-done | bytes 262176 | tf_op jit(solution)/shard_map/ppermute | solution.py:341
  57.5 0.0 collective-permute-done.15.refs_2_
  57.6 0.5 collective-permute-start.16
  58.1 1.9 %collective-permute-done.18.refs_6_ = bf16[128,1024]{1,0:T(8,128)(2,1)S(1)} collective-permute-done((bf16[128,1024]{1,0:T(8,128)(2,1)S(1)}, bf16[128,1024]{1,0:T(8,128)(2,1)S(1)}, u32[]{:S(2)}, u32[]{:S(2)}) %collective-permute-start.18) | collective-permute-done | bytes 262176 | tf_op jit(solution)/shard_map/ppermute | solution.py:341
  60.0 0.3 collective-permute-start.19
  60.3 3.6 %collective-permute-done.9.refs_5_ = bf16[128,1024]{1,0:T(8,128)(2,1)S(1)} collective-permute-done((bf16[128,1024]{1,0:T(8,128)(2,1)S(1)}, bf16[128,1024]{1,0:T(8,128)(2,1)S(1)}, u32[]{:S(2)}, u32[]{:S(2)}) %collective-permute-start.9) | collective-permute-done | bytes 262176 | tf_op jit(solution)/shard_map/ppermute | solution.py:341
  63.9 0.0 collective-permute-start.10
  63.9 0.0 collective-permute-done.20.refs_0_
  63.9 0.5 collective-permute-start.3
  64.4 3.4 %copy-done.1 = bf16[2048,2048]{1,0:T(8,128)(2,1)S(1)} copy-done((bf16[2048,2048]{1,0:T(8,128)(2,1)S(1)}, bf16[2048,2048]{1,0:T(8,128)(2,1)}, u32[]{:S(2)}) %copy-start.1) | copy-done | bytes 8388632
  67.8 3.4 %shard_map.64 = (bf16[2048,2048]{1,0:T(8,128)(2,1)S(1)}, bf16[512,2048]{1,0:T(8,128)(2,1)S(1)}, f32[512,2048]{1,0:T(8,128)S(1)}) custom-call(bf16[512,1024]{1,0:T(8,128)(2,1)S(1)} %collective-permute-done.20.refs_0_, bf16[128,1024]{1,0:T(8,128)(2,1)S(1)} %collective-permute-done.5.refs_1_, ...), custom_call_target="tpu_custom_call", output_to_operand_aliasing={{0}: (15, {})} | custom-call | tf_op jit(solution)/shard_map/pallas_call | solution.py:402
  71.2 0.0 collective-permute-done.16.refs_3_
  71.2 0.0 collective-permute-done.19.refs_7_
  71.2 0.0 copy-start.3
  71.2 0.0 copy-start.5
  71.2 0.0 copy-start.6
  71.2 0.0 copy-start.7
  71.2 2.9 %shard_map.65 = (bf16[2048,2048]{1,0:T(8,128)(2,1)S(1)}, f32[512,2048]{1,0:T(8,128)S(1)}) custom-call(bf16[128,1024]{1,0:T(8,128)(2,1)S(1)} %collective-permute-done.11.refs_0_, bf16[128,1024]{1,0:T(8,128)(2,1)S(1)} %collective-permute-done.12.refs_1_, ...), custom_call_target="tpu_custom_call", output_to_operand_aliasing={{0}: (8, {}), {1}: (9, {})} | custom-call | tf_op jit(solution)/shard_map/pallas_call | solution.py:402
  74.2 0.0 collective-permute-done.3.refs_4_
  74.2 0.0 collective-permute-done.10.refs_6_
  74.2 7.0 %force.1 = (f32[3,8]{1,0:T(4,128)}, bf16[2048,2048]{1,0:T(8,128)(2,1)S(1)}) custom-call(s32[32]{0:T(128)S(1)} %bitcast.1, s32[32]{0:T(128)S(1)} %copy-done.6, s32[32]{0:T(128)S(1)} %copy-done.7, s32[4,4,8]{2,1,0:T(4,128)S(1)} %get-tuple-element.15.refs_3_, s32[4,4,8]{2,1,0:T(4,128)S(1)} %collective-permute-done.3.refs_4_, ...), custom_call_target="tpu_custom_call", output_to_operand_aliasing={{1}: (7, {})} | custom-call | tf_op jit(solution)/shard_map/force/pallas_call | solution.py:422
  (21 shorter events, 0.1 us)
Async XLA Ops:
  1.7 21.0 %collective-permute-start.5 = (bf16[128,1024]{1,0:T(8,128)(2,1)}, bf16[128,1024]{1,0:T(8,128)(2,1)S(1)}, u32[]{:S(2)}, u32[]{:S(2)}) collective-permute-start(bf16[128,1024]{1,0:T(8,128)(2,1)} %unit.1), channel_id=1, source_target_pairs={{0,2},{2,0},{4,6},{6,4},{1,3},{3,1},{5,7},{7,5},{8,10},{10,8},{12,... | collective-permute-start | bytes 786440 | tf_op jit(solution)/shard_map/ppermute | solution.py:333
  4.9 18.6 %collective-permute-start.4 = (bf16[128,1024]{1,0:T(8,128)(2,1)}, bf16[128,1024]{1,0:T(8,128)(2,1)S(1)}, u32[]{:S(2)}, u32[]{:S(2)}) collective-permute-start(bf16[128,1024]{1,0:T(8,128)(2,1)} %unit.1), channel_id=1, source_target_pairs={{2,4},{4,2},{3,5},{5,3},{10,12},{12,10},{11,13},{13,11},{18,20},{2... | collective-permute-start | bytes 786440 | tf_op jit(solution)/shard_map/ppermute | solution.py:333
  5.5 6.8 %collective-permute-start = (s32[4,8]{1,0:T(4,128)}, s32[4,8]{1,0:T(4,128)S(1)}, u32[]{:S(2)}, u32[]{:S(2)}) collective-permute-start(s32[4,8]{1,0:T(4,128)} %source_ref.1), channel_id=1, source_target_pairs={{0,2},{2,0},{4,6},{6,4},{1,3},{3,1},{5,7},{7,5},{8,10},{10,8},{12,... | collective-permute-start | bytes 392 | tf_op jit(solution)/shard_map/ppermute | solution.py:333
  9.9 5.8 %collective-permute-start.1 = (s32[4,8]{1,0:T(4,128)}, s32[4,8]{1,0:T(4,128)S(1)}, u32[]{:S(2)}, u32[]{:S(2)}) collective-permute-start(s32[4,8]{1,0:T(4,128)} %source_ref.1), channel_id=1, source_target_pairs={{0,4},{2,6},{4,0},{6,2},{1,5},{3,7},{5,1},{7,3},{8,12},{10,14},{12... | collective-permute-start | bytes 392 | tf_op jit(solution)/shard_map/ppermute | solution.py:333
  9.9 5.8 %collective-permute-start.2 = (s32[4,8]{1,0:T(4,128)}, s32[4,8]{1,0:T(4,128)S(1)}, u32[]{:S(2)}, u32[]{:S(2)}) collective-permute-start(s32[4,8]{1,0:T(4,128)} %source_ref.1), channel_id=1, source_target_pairs={{0,6},{2,4},{4,2},{6,0},{1,7},{3,5},{5,3},{7,1},{8,14},{10,12},{12... | collective-permute-start | bytes 392 | tf_op jit(solution)/shard_map/ppermute | solution.py:333
  15.7 1.2 %copy-start.2 = (bf16[512,1024]{1,0:T(8,128)(2,1)S(1)}, bf16[512,1024]{1,0:T(8,128)(2,1)}, u32[]{:S(2)}) copy-start(bf16[512,1024]{1,0:T(8,128)(2,1)} %density_ref.3) | copy-start | bytes 3145732
  16.9 0.7 copy-start.4
  18.9 3.3 %copy-start = (bf16[2048,2048]{1,0:T(8,128)(2,1)}, bf16[2048,2048]{1,0:T(8,128)(2,1)S(1)}, u32[]{:S(2)}) copy-start(bf16[2048,2048]{1,0:T(8,128)(2,1)S(1)} %get-tuple-element.18.refs_15_) | copy-start | bytes 25165828
  22.2 8.1 %collective-permute-start.11 = (bf16[128,1024]{1,0:T(8,128)(2,1)S(1)}, bf16[128,1024]{1,0:T(8,128)(2,1)S(1)}, u32[]{:S(2)}, u32[]{:S(2)}) collective-permute-start(bf16[128,1024]{1,0:T(8,128)(2,1)S(1)} %get-tuple-element.16), channel_id=1, source_target_pairs={{0,2},{2,0},{4,6},{6,4},{1,3},{3,1},{5,7},{7,5},{8,10},{10,8},{12,... | collective-permute-start | bytes 786440 | tf_op jit(solution)/shard_map/ppermute | solution.py:333
  22.8 7.5 %collective-permute-start.6 = (bf16[128,1024]{1,0:T(8,128)(2,1)S(1)}, bf16[128,1024]{1,0:T(8,128)(2,1)S(1)}, u32[]{:S(2)}, u32[]{:S(2)}) collective-permute-start(bf16[128,1024]{1,0:T(8,128)(2,1)S(1)} %collective-permute-done.5.refs_1_), channel_id=1, source_target_pairs={{2,4},{4,2},{3,5},{5,3},{10,12},{12,10},{11,13},{13,11},{18,20},{2... | collective-permute-start | bytes 786440 | tf_op jit(solution)/shard_map/ppermute | solution.py:333
  23.4 11.2 %collective-permute-start.13 = (bf16[128,1024]{1,0:T(8,128)(2,1)S(1)}, bf16[128,1024]{1,0:T(8,128)(2,1)S(1)}, u32[]{:S(2)}, u32[]{:S(2)}) collective-permute-start(bf16[128,1024]{1,0:T(8,128)(2,1)S(1)} %collective-permute-done.4), channel_id=1, source_target_pairs={{2,0},{4,6},{3,1},{5,7},{10,8},{12,14},{11,9},{13,15},{18,16},{20,... | collective-permute-start | bytes 786440 | tf_op jit(solution)/shard_map/ppermute | solution.py:333
  24.8 11.5 %collective-permute-start.22 = (bf16[128,1024]{1,0:T(8,128)(2,1)S(1)}, bf16[128,1024]{1,0:T(8,128)(2,1)S(1)}, u32[]{:S(2)}, u32[]{:S(2)}) collective-permute-start(bf16[128,1024]{1,0:T(8,128)(2,1)S(1)} %collective-permute-done.5.refs_1_), channel_id=1, source_target_pairs={{0,8},{1,17},{8,0},{9,25},{16,24},{17,1},{24,16},{25,9},{2,10},{3,... | collective-permute-start | bytes 786440 | tf_op jit(solution)/shard_map/ppermute | solution.py:341
  26.3 11.4 %collective-permute-start.24 = (bf16[128,1024]{1,0:T(8,128)(2,1)S(1)}, bf16[128,1024]{1,0:T(8,128)(2,1)S(1)}, u32[]{:S(2)}, u32[]{:S(2)}) collective-permute-start(bf16[128,1024]{1,0:T(8,128)(2,1)S(1)} %collective-permute-done.5.refs_1_), channel_id=1, source_target_pairs={{0,16},{1,9},{8,24},{9,1},{16,0},{17,25},{24,8},{25,17},{2,18},{3,... | collective-permute-start | bytes 786440 | tf_op jit(solution)/shard_map/ppermute | solution.py:341
  30.2 7.5 %collective-permute-start.21 = (bf16[128,1024]{1,0:T(8,128)(2,1)S(1)}, bf16[128,1024]{1,0:T(8,128)(2,1)S(1)}, u32[]{:S(2)}, u32[]{:S(2)}) collective-permute-start(bf16[128,1024]{1,0:T(8,128)(2,1)S(1)} %collective-permute-done.5.refs_1_), channel_id=1, source_target_pairs={{0,1},{1,0},{2,3},{3,2},{4,5},{5,4},{6,7},{7,6},{8,9},{9,8},{10,11... | collective-permute-start | bytes 786440 | tf_op jit(solution)/shard_map/ppermute | solution.py:333
  30.2 8.8 %collective-permute-start.12 = (bf16[128,1024]{1,0:T(8,128)(2,1)S(1)}, bf16[128,1024]{1,0:T(8,128)(2,1)S(1)}, u32[]{:S(2)}, u32[]{:S(2)}) collective-permute-start(bf16[128,1024]{1,0:T(8,128)(2,1)S(1)} %collective-permute-done.11.refs_0_), channel_id=1, source_target_pairs={{0,1},{1,0},{2,3},{3,2},{4,5},{5,4},{6,7},{7,6},{8,9},{9,8},{10,11... | collective-permute-start | bytes 786440 | tf_op jit(solution)/shard_map/ppermute | solution.py:333
  34.7 8.0 %collective-permute-start.14 = (bf16[128,1024]{1,0:T(8,128)(2,1)S(1)}, bf16[128,1024]{1,0:T(8,128)(2,1)S(1)}, u32[]{:S(2)}, u32[]{:S(2)}) collective-permute-start(bf16[128,1024]{1,0:T(8,128)(2,1)S(1)} %broadcast_select_fusion.refs_7_), channel_id=1, source_target_pairs={{0,8},{1,17},{8,0},{9,25},{16,24},{17,1},{24,16},{25,9},{2,10},{3,... | collective-permute-start | bytes 786440 | tf_op jit(solution)/shard_map/ppermute | solution.py:341
  36.2 6.4 %collective-permute-start.28 = (bf16[128,1024]{1,0:T(8,128)(2,1)S(1)}, bf16[128,1024]{1,0:T(8,128)(2,1)S(1)}, u32[]{:S(2)}, u32[]{:S(2)}) collective-permute-start(bf16[128,1024]{1,0:T(8,128)(2,1)S(1)} %broadcast_select_fusion.refs_7_), channel_id=1, source_target_pairs={{0,16},{1,9},{8,24},{9,1},{16,0},{17,25},{24,8},{25,17},{2,18},{3,... | collective-permute-start | bytes 786440 | tf_op jit(solution)/shard_map/ppermute | solution.py:341
  37.7 5.4 %collective-permute-start.26 = (bf16[128,1024]{1,0:T(8,128)(2,1)S(1)}, bf16[128,1024]{1,0:T(8,128)(2,1)S(1)}, u32[]{:S(2)}, u32[]{:S(2)}) collective-permute-start(bf16[128,1024]{1,0:T(8,128)(2,1)S(1)} %broadcast_select_fusion.refs_7_), channel_id=1, source_target_pairs={{0,1},{1,0},{2,3},{3,2},{4,5},{5,4},{6,7},{7,6},{8,9},{9,8},{10,11... | collective-permute-start | bytes 786440 | tf_op jit(solution)/shard_map/ppermute | solution.py:333
  37.7 10.6 %collective-permute-start.7 = (bf16[128,1024]{1,0:T(8,128)(2,1)S(1)}, bf16[128,1024]{1,0:T(8,128)(2,1)S(1)}, u32[]{:S(2)}, u32[]{:S(2)}) collective-permute-start(bf16[128,1024]{1,0:T(8,128)(2,1)S(1)} %collective-permute-done.6), channel_id=1, source_target_pairs={{2,0},{4,6},{3,1},{5,7},{10,8},{12,14},{11,9},{13,15},{18,16},{20,... | collective-permute-start | bytes 786440 | tf_op jit(solution)/shard_map/ppermute | solution.py:333
  39.0 24.9 %collective-permute-start.20 = (bf16[512,1024]{1,0:T(8,128)(2,1)S(1)}, bf16[512,1024]{1,0:T(8,128)(2,1)S(1)}, u32[]{:S(2)}, u32[]{:S(2)}) collective-permute-start(bf16[512,1024]{1,0:T(8,128)(2,1)S(1)} %get-tuple-element.17), channel_id=1, source_target_pairs={{0,1},{1,0},{2,3},{3,2},{4,5},{5,4},{6,7},{7,6},{8,9},{9,8},{10,11... | collective-permute-start | bytes 3145736 | tf_op jit(solution)/shard_map/ppermute | solution.py:333
  42.7 5.7 %collective-permute-start.23 = (bf16[128,1024]{1,0:T(8,128)(2,1)S(1)}, bf16[128,1024]{1,0:T(8,128)(2,1)S(1)}, u32[]{:S(2)}, u32[]{:S(2)}) collective-permute-start(bf16[128,1024]{1,0:T(8,128)(2,1)S(1)} %collective-permute-done.22.refs_3_), channel_id=1, source_target_pairs={{0,1},{1,0},{2,3},{3,2},{4,5},{5,4},{6,7},{7,6},{8,9},{9,8},{10,11... | collective-permute-start | bytes 786440 | tf_op jit(solution)/shard_map/ppermute | solution.py:333
  42.7 6.3 %collective-permute-start.25 = (bf16[128,1024]{1,0:T(8,128)(2,1)S(1)}, bf16[128,1024]{1,0:T(8,128)(2,1)S(1)}, u32[]{:S(2)}, u32[]{:S(2)}) collective-permute-start(bf16[128,1024]{1,0:T(8,128)(2,1)S(1)} %collective-permute-done.24.refs_5_), channel_id=1, source_target_pairs={{0,1},{1,0},{2,3},{3,2},{4,5},{5,4},{6,7},{7,6},{8,9},{9,8},{10,11... | collective-permute-start | bytes 786440 | tf_op jit(solution)/shard_map/ppermute | solution.py:333
  43.2 6.0 %collective-permute-start.27 = (bf16[128,1024]{1,0:T(8,128)(2,1)S(1)}, bf16[128,1024]{1,0:T(8,128)(2,1)S(1)}, u32[]{:S(2)}, u32[]{:S(2)}) collective-permute-start(bf16[128,1024]{1,0:T(8,128)(2,1)S(1)} %collective-permute-done.14.refs_9_), channel_id=1, source_target_pairs={{0,1},{1,0},{2,3},{3,2},{4,5},{5,4},{6,7},{7,6},{8,9},{9,8},{10,11... | collective-permute-start | bytes 786440 | tf_op jit(solution)/shard_map/ppermute | solution.py:333
  48.3 2.4 %collective-permute-start.29 = (bf16[128,1024]{1,0:T(8,128)(2,1)S(1)}, bf16[128,1024]{1,0:T(8,128)(2,1)S(1)}, u32[]{:S(2)}, u32[]{:S(2)}) collective-permute-start(bf16[128,1024]{1,0:T(8,128)(2,1)S(1)} %collective-permute-done.28.refs_11_), channel_id=1, source_target_pairs={{0,1},{1,0},{2,3},{3,2},{4,5},{5,4},{6,7},{7,6},{8,9},{9,8},{10,11... | collective-permute-start | bytes 786440 | tf_op jit(solution)/shard_map/ppermute | solution.py:333
  48.4 9.1 %collective-permute-start.8 = (bf16[128,1024]{1,0:T(8,128)(2,1)S(1)}, bf16[128,1024]{1,0:T(8,128)(2,1)S(1)}, u32[]{:S(2)}, u32[]{:S(2)}) collective-permute-start(bf16[128,1024]{1,0:T(8,128)(2,1)S(1)} %broadcast_select_fusion.1.refs_13_), channel_id=1, source_target_pairs={{0,8},{1,17},{8,0},{9,25},{16,24},{17,1},{24,16},{25,9},{2,10},{3,... | collective-permute-start | bytes 786440 | tf_op jit(solution)/shard_map/ppermute | solution.py:341
  49.0 8.5 %collective-permute-start.30 = (bf16[128,1024]{1,0:T(8,128)(2,1)S(1)}, bf16[128,1024]{1,0:T(8,128)(2,1)S(1)}, u32[]{:S(2)}, u32[]{:S(2)}) collective-permute-start(bf16[128,1024]{1,0:T(8,128)(2,1)S(1)} %broadcast_select_fusion.1.refs_13_), channel_id=1, source_target_pairs={{0,1},{1,0},{2,3},{3,2},{4,5},{5,4},{6,7},{7,6},{8,9},{9,8},{10,11... | collective-permute-start | bytes 786440 | tf_op jit(solution)/shard_map/ppermute | solution.py:333
  49.2 8.3 %collective-permute-start.15 = (bf16[128,1024]{1,0:T(8,128)(2,1)S(1)}, bf16[128,1024]{1,0:T(8,128)(2,1)S(1)}, u32[]{:S(2)}, u32[]{:S(2)}) collective-permute-start(bf16[128,1024]{1,0:T(8,128)(2,1)S(1)} %collective-permute-done.14.refs_9_), channel_id=1, source_target_pairs={{0,16},{1,9},{8,24},{9,1},{16,0},{17,25},{24,8},{25,17},{2,18},{3,... | collective-permute-start | bytes 786440 | tf_op jit(solution)/shard_map/ppermute | solution.py:341
  50.7 9.3 %collective-permute-start.18 = (bf16[128,1024]{1,0:T(8,128)(2,1)S(1)}, bf16[128,1024]{1,0:T(8,128)(2,1)S(1)}, u32[]{:S(2)}, u32[]{:S(2)}) collective-permute-start(bf16[128,1024]{1,0:T(8,128)(2,1)S(1)} %broadcast_select_fusion.1.refs_13_), channel_id=1, source_target_pairs={{0,16},{1,9},{8,24},{9,1},{16,0},{17,25},{24,8},{25,17},{2,18},{3,... | collective-permute-start | bytes 786440 | tf_op jit(solution)/shard_map/ppermute | solution.py:341
  57.5 6.4 %collective-permute-start.9 = (bf16[128,1024]{1,0:T(8,128)(2,1)S(1)}, bf16[128,1024]{1,0:T(8,128)(2,1)S(1)}, u32[]{:S(2)}, u32[]{:S(2)}) collective-permute-start(bf16[128,1024]{1,0:T(8,128)(2,1)S(1)} %collective-permute-done.8.refs_4_), channel_id=1, source_target_pairs={{0,16},{1,9},{8,24},{9,1},{16,0},{17,25},{24,8},{25,17},{2,18},{3,... | collective-permute-start | bytes 786440 | tf_op jit(solution)/shard_map/ppermute | solution.py:341
  57.5 13.6 %collective-permute-start.17 = (bf16[128,1024]{1,0:T(8,128)(2,1)S(1)}, bf16[128,1024]{1,0:T(8,128)(2,1)S(1)}, u32[]{:S(2)}, u32[]{:S(2)}) collective-permute-start(bf16[128,1024]{1,0:T(8,128)(2,1)S(1)} %collective-permute-done.8.refs_4_), channel_id=1, source_target_pairs={{0,1},{1,0},{2,3},{3,2},{4,5},{5,4},{6,7},{7,6},{8,9},{9,8},{10,11... | collective-permute-start | bytes 786440 | tf_op jit(solution)/shard_map/ppermute | solution.py:333
  57.6 13.6 %collective-permute-start.16 = (bf16[128,1024]{1,0:T(8,128)(2,1)S(1)}, bf16[128,1024]{1,0:T(8,128)(2,1)S(1)}, u32[]{:S(2)}, u32[]{:S(2)}) collective-permute-start(bf16[128,1024]{1,0:T(8,128)(2,1)S(1)} %collective-permute-done.15.refs_2_), channel_id=1, source_target_pairs={{0,1},{1,0},{2,3},{3,2},{4,5},{5,4},{6,7},{7,6},{8,9},{9,8},{10,11... | collective-permute-start | bytes 786440 | tf_op jit(solution)/shard_map/ppermute | solution.py:333
  60.0 11.2 %collective-permute-start.19 = (bf16[128,1024]{1,0:T(8,128)(2,1)S(1)}, bf16[128,1024]{1,0:T(8,128)(2,1)S(1)}, u32[]{:S(2)}, u32[]{:S(2)}) collective-permute-start(bf16[128,1024]{1,0:T(8,128)(2,1)S(1)} %collective-permute-done.18.refs_6_), channel_id=1, source_target_pairs={{0,1},{1,0},{2,3},{3,2},{4,5},{5,4},{6,7},{7,6},{8,9},{9,8},{10,11... | collective-permute-start | bytes 786440 | tf_op jit(solution)/shard_map/ppermute | solution.py:333
  63.9 10.3 %collective-permute-start.10 = (bf16[128,1024]{1,0:T(8,128)(2,1)S(1)}, bf16[128,1024]{1,0:T(8,128)(2,1)S(1)}, u32[]{:S(2)}, u32[]{:S(2)}) collective-permute-start(bf16[128,1024]{1,0:T(8,128)(2,1)S(1)} %collective-permute-done.9.refs_5_), channel_id=1, source_target_pairs={{0,1},{1,0},{2,3},{3,2},{4,5},{5,4},{6,7},{7,6},{8,9},{9,8},{10,11... | collective-permute-start | bytes 786440 | tf_op jit(solution)/shard_map/ppermute | solution.py:333
  63.9 10.2 %collective-permute-start.3 = (s32[4,4,8]{2,1,0:T(4,128)S(1)}, s32[4,4,8]{2,1,0:T(4,128)S(1)}, u32[]{:S(2)}, u32[]{:S(2)}) collective-permute-start(s32[4,4,8]{2,1,0:T(4,128)S(1)} %get-tuple-element.15.refs_3_), channel_id=1, source_target_pairs={{0,1},{1,0},{2,3},{3,2},{4,5},{5,4},{6,7},{7,6},{8,9},{9,8},{10,11... | collective-permute-start | bytes 1544 | tf_op jit(solution)/shard_map/ppermute | solution.py:333
  64.4 3.4 %copy-start.1 = (bf16[2048,2048]{1,0:T(8,128)(2,1)S(1)}, bf16[2048,2048]{1,0:T(8,128)(2,1)}, u32[]{:S(2)}) copy-start(bf16[2048,2048]{1,0:T(8,128)(2,1)} %copy-done) | copy-start | bytes 25165828
  71.2 3.0 %copy-start.3 = (bf16[32,3,128,128]{3,2,1,0:T(8,128)(2,1)S(1)}, bf16[32,3,128,128]{3,2,1,0:T(8,128)(2,1)}, u32[]{:S(2)}) copy-start(bf16[32,3,128,128]{3,2,1,0:T(8,128)(2,1)} %refs_10_.1) | copy-start | bytes 9437188
  71.2 3.0 %copy-start.5 = (s32[32,1]{0,1:T(1,128)S(1)}, s32[32,1]{0,1:T(1,128)}, u32[]{:S(2)}) copy-start(s32[32,1]{0,1:T(1,128)} %param.8) | copy-start | bytes 388
  71.2 3.0 %copy-start.6 = (s32[32]{0:T(128)S(1)}, s32[32]{0:T(128)}, u32[]{:S(2)}) copy-start(s32[32]{0:T(128)} %refs_1_.1) | copy-start | bytes 388
  71.2 3.0 %copy-start.7 = (s32[32]{0:T(128)S(1)}, s32[32]{0:T(128)}, u32[]{:S(2)}) copy-start(s32[32]{0:T(128)} %refs_2_.1) | copy-start | bytes 388
